TPU v7x, 32 devices: a whole 2x2x4 slice. The times are simulated.
32 devices in a mesh: long: 8 (over y, x, core), short: 4 (over z).
Axes of the slice: x: 2, y: 2, z: 4, core: 2. Of those that a mesh axis runs over, the one named last changes fastest.
Arguments:
- transition: float32 [64, 384, 384], P(('long', 'short')), may hold values from 0 to 1
- innovation: float32 [64, 384], P(('long', 'short')), may hold values from 20 to 80
- observation: float32 [64, 384], P(('long', 'short')), may hold values from 0.05 to 0.5
- effects: float32 [64, 384, 384], P(('long', 'short')), may hold values from -0.0045 to 0.0045
- prior: float32 [384], replicated, may hold values from 0.5 to 2
- right_side: float32 [64, 384, 128], P(('long', 'short')), may hold values from -3 to 3
- tip_right: float32 [384, 128], replicated, may hold values from -6 to 6
Outputs:
- solution: float32 [64, 384, 128], P(('long', 'short'))
- tip_solution: float32 [384, 128], replicated
All inputs are finite; a program needn't handle non-finite values.
Results may differ from a plain program's by a relative error of at most 0.0003.
Values sent between devices are 32-bit elements; how exact they have to be, the bound alone decides.
A program may use at most 256 MiB of HBM per device.

v0:
```python
import jax
import jax.numpy as jnp
from jax import lax
from jax.sharding import PartitionSpec as P

HIGHEST = lax.Precision.HIGHEST


def shifted(block, axis, distance):
    devices = range(lax.axis_size(axis))
    route = [(i - distance, i) for i in devices if i - distance in devices]
    return lax.ppermute(block, axis, route)


def gram_prod(left, right):
    return jnp.einsum("ji,jk->ik", left, right, precision=HIGHEST)


def mat_prod(left, right):
    return jnp.matmul(left, right, precision=HIGHEST)


def solve_lower(factor, values):
    return jax.scipy.linalg.solve_triangular(factor, values, lower=True)


def solve_upper(factor, values):
    return jax.scipy.linalg.solve_triangular(factor, values, lower=True, trans=1)


def move_near(values, offset):
    return shifted(values, ("long", "short"), offset)


def move_far(values, offset):
    return shifted(values, "long", offset)


def reduce_level(state, distance, index, total, active, mover, tip_width):
    node_diag, node_couple, node_arrow, node_rhs, tip_terms, tip_rhs_terms = state
    node_width = node_diag.shape[0]
    side_count = node_rhs.shape[1]
    rank_one = index + 1
    alive = jnp.logical_and(active, rank_one % distance == 0)
    drop = jnp.logical_and(alive, rank_one // distance % 2 == 1)
    keep = jnp.logical_and(alive, jnp.logical_not(drop))
    from_left = jnp.logical_and(keep, index - distance >= 0)
    from_right = jnp.logical_and(keep, index + distance <= total - 1)
    identity = jnp.eye(node_width, dtype=jnp.float32)
    full_width = 2 * node_width + tip_width + side_count
    part_width = node_width + tip_width + side_count
    tip_zero = jnp.zeros((tip_width, tip_width + side_count), jnp.float32)
    right_couple = mover(node_couple, -distance)

    def eliminate(operands):
        diag_item, couple_item, right_item, arrow_item, rhs_item = operands
        factor = jnp.linalg.cholesky(diag_item)
        solved = solve_lower(
            factor, jnp.concatenate([couple_item, right_item.T, arrow_item, rhs_item], axis=1)
        )
        part_left = solved[:, :node_width]
        rest = solved[:, 2 * node_width :]
        toward_left = gram_prod(part_left, jnp.concatenate([part_left, rest], axis=1))
        toward_right = gram_prod(solved[:, node_width : 2 * node_width], solved)
        tip_part = gram_prod(rest[:, :tip_width], rest)
        return (factor, solved, toward_left, toward_right, tip_part)

    def skip(operands):
        return (
            identity,
            jnp.zeros((node_width, full_width), jnp.float32),
            jnp.zeros((node_width, part_width), jnp.float32),
            jnp.zeros((node_width, full_width), jnp.float32),
            tip_zero,
        )

    factor, solved, toward_left, toward_right, tip_part = lax.cond(
        drop, eliminate, skip, (node_diag, node_couple, right_couple, node_arrow, node_rhs)
    )
    left_update = mover(toward_right, distance)
    saved = (
        factor,
        solved[:, :node_width],
        solved[:, node_width : 2 * node_width],
        solved[:, 2 * node_width : 2 * node_width + tip_width],
        solved[:, 2 * node_width + tip_width :],
        None,
        drop,
    )
    right_update = mover(toward_left, -distance)
    right_gate = jnp.where(from_right, 1.0, 0.0)
    left_gate = jnp.where(from_left, 1.0, 0.0)
    arrow_end = 2 * node_width + tip_width
    node_diag = (
        node_diag
        - right_gate * right_update[:, :node_width]
        - left_gate * left_update[:, node_width : 2 * node_width]
    )
    node_couple = jnp.where(from_left, -left_update[:, :node_width], node_couple)
    node_arrow = (
        node_arrow
        - right_gate * right_update[:, node_width : node_width + tip_width]
        - left_gate * left_update[:, 2 * node_width : arrow_end]
    )
    node_rhs = (
        node_rhs
        - right_gate * right_update[:, node_width + tip_width :]
        - left_gate * left_update[:, arrow_end:]
    )
    tip_terms = tip_terms - tip_part[:, :tip_width]
    tip_rhs_terms = tip_rhs_terms - tip_part[:, tip_width:]
    return ((node_diag, node_couple, node_arrow, node_rhs, tip_terms, tip_rhs_terms), saved)


def unwind_level(node_x, saved, tip_solution, mover, distance):
    factor, part_left, part_right, part_arrow, part_rhs, link, drop = saved
    left_x = mover(node_x, distance)
    right_term = mat_prod(part_right, mover(node_x, -distance))
    value = part_rhs - mat_prod(part_left, left_x) - right_term - mat_prod(part_arrow, tip_solution)
    return jnp.where(drop, solve_upper(factor, value), node_x)


def body(transition, innovation, observation, effects, prior, right_side, tip_right):
    block_count, node_width = innovation.shape
    tip_width = prior.shape[0]
    side_count = right_side.shape[2]
    device_count = lax.axis_size(("long", "short"))
    short_count = lax.axis_size("short")
    long_count = lax.axis_size("long")
    position = lax.axis_index(("long", "short"))
    long_place = lax.axis_index("long")
    short_place = lax.axis_index("short")
    identity = jnp.eye(node_width, dtype=jnp.float32)
    weighted_trans = innovation[:, :, None] * transition
    weighted_effect = innovation[:, :, None] * effects
    succ_diag = jnp.einsum("tji,tjk->tik", transition, weighted_trans, precision=HIGHEST)
    succ_arrow = jnp.einsum("tji,tjk->tik", transition, weighted_effect, precision=HIGHEST)
    tip_terms = jnp.einsum("tji,tjk->ik", effects, weighted_effect, precision=HIGHEST)
    global_block = position * block_count + jnp.arange(block_count)
    couple = -weighted_trans * jnp.where(global_block == 0, 0.0, 1.0)[:, None, None]
    diag_base = (innovation + observation)[:, :, None] * identity
    interior = block_count - 1
    own_diag = diag_base[:interior] + succ_diag[1:]
    own_arrow = -weighted_effect[:interior] + succ_arrow[1:]
    order = jnp.arange(interior)
    first = (order == 0)[:, None, None]
    last = (order == interior - 1)[:, None, None]
    left_cols = jnp.where(first, couple[0][None], 0.0)
    sep_cols = jnp.where(last, couple[interior].T[None], 0.0)
    previous = jnp.where(first, 0.0, couple[:interior])
    columns = jnp.concatenate([left_cols, sep_cols, own_arrow, right_side[:interior]], axis=2)
    span = 2 * node_width + tip_width
    full_width = span + side_count

    def forward(carry, items):
        factor_prev, solved_prev, gram = carry
        diag_item, prev_item, column_item = items
        link = solve_lower(factor_prev, prev_item.T)
        factor = jnp.linalg.cholesky(diag_item - gram_prod(link, link))
        solved = solve_lower(factor, column_item - gram_prod(link, solved_prev))
        gram = gram + gram_prod(solved[:, :span], solved)
        return ((factor, solved, gram), (factor, link, solved))

    start = (
        identity,
        jnp.zeros((node_width, full_width), jnp.float32),
        jnp.zeros((span, full_width), jnp.float32),
    )
    final_carry, stored = lax.scan(forward, start, (own_diag, previous, columns))
    gram = final_carry[2]
    factors, links, solved_all = stored
    left_rows = gram[:node_width]
    sep_rows = gram[node_width : 2 * node_width]
    tip_rows = gram[2 * node_width :]
    left_terms = (
        -left_rows[:, :node_width],
        -left_rows[:, 2 * node_width : span],
        -left_rows[:, span:],
    )
    tip_terms = tip_terms - tip_rows[:, 2 * node_width : span]
    tip_rhs_terms = -tip_rows[:, span:]
    recv_diag, recv_arrow, recv_rhs = move_near(
        (left_terms[0] + succ_diag[0], left_terms[1] + succ_arrow[0], left_terms[2]), -1
    )
    node_diag = diag_base[interior] - sep_rows[:, node_width : 2 * node_width] + recv_diag
    node_couple = -sep_rows[:, :node_width]
    node_arrow = -weighted_effect[interior] - sep_rows[:, 2 * node_width : span] + recv_arrow
    node_rhs = right_side[interior] - sep_rows[:, span:] + recv_rhs
    state = (node_diag, node_couple, node_arrow, node_rhs, tip_terms, tip_rhs_terms)
    always = position >= 0
    lower_saved = []
    for depth in range(short_count.bit_length() - 1):
        state, saved = reduce_level(
            state, 2**depth, position, device_count, always, move_near, tip_width
        )
        lower_saved.append(saved)
    top_row = short_place == short_count - 1
    upper_saved = []
    for depth in range(long_count.bit_length() - 1):
        state, saved = reduce_level(
            state, 2**depth, long_place, long_count, top_row, move_far, tip_width
        )
        upper_saved.append(saved)
    node_diag, node_couple, node_arrow, node_rhs, tip_terms, tip_rhs_terms = state
    final = position == device_count - 1

    def finish(operands):
        diag_item, arrow_item, rhs_item = operands
        factor = jnp.linalg.cholesky(diag_item)
        solved = solve_lower(factor, jnp.concatenate([arrow_item, rhs_item], axis=1))
        return (factor, solved, gram_prod(solved[:, :tip_width], solved))

    def pass_over(operands):
        return (
            identity,
            jnp.zeros((node_width, tip_width + side_count), jnp.float32),
            jnp.zeros((tip_width, tip_width + side_count), jnp.float32),
        )

    final_factor, final_solved, final_tip = lax.cond(
        final, finish, pass_over, (node_diag, node_arrow, node_rhs)
    )
    tip_terms = tip_terms - final_tip[:, :tip_width]
    tip_rhs_terms = tip_rhs_terms - final_tip[:, tip_width:]
    tip_total, tip_rhs_total = lax.psum((tip_terms, tip_rhs_terms), ("long", "short"))
    tip_factor = jnp.linalg.cholesky(tip_total + jnp.diag(prior))
    tip_solution = solve_upper(tip_factor, solve_lower(tip_factor, tip_rhs_total + tip_right))
    final_x = solve_upper(
        final_factor,
        final_solved[:, tip_width:] - mat_prod(final_solved[:, :tip_width], tip_solution),
    )
    node_x = jnp.where(final, final_x, jnp.zeros_like(final_x))
    for depth in reversed(range(len(upper_saved))):
        node_x = unwind_level(node_x, upper_saved[depth], tip_solution, move_far, 2**depth)
    for depth in reversed(range(len(lower_saved))):
        node_x = unwind_level(node_x, lower_saved[depth], tip_solution, move_near, 2**depth)
    left_x = move_near(node_x, 1)
    next_links = jnp.concatenate(
        [links[1:], jnp.zeros((1, node_width, node_width), jnp.float32)], axis=0
    )

    def backward(later, items):
        factor, link_next, solved = items
        value = (
            solved[:, span:]
            - mat_prod(solved[:, :node_width], left_x)
            - mat_prod(solved[:, node_width : 2 * node_width], node_x)
            - mat_prod(solved[:, 2 * node_width : span], tip_solution)
            - mat_prod(link_next, later)
        )
        current = solve_upper(factor, value)
        return (current, current)

    last_value, interior_x = lax.scan(
        backward,
        jnp.zeros((node_width, side_count), jnp.float32),
        (factors, next_links, solved_all),
        reverse=True,
    )
    solution = jnp.concatenate([interior_x, node_x[None]], axis=0)
    return (solution, tip_solution)


def solution(mesh):
    placed = (
        P(("long", "short"), None, None),
        P(("long", "short"), None),
        P(("long", "short"), None),
        P(("long", "short"), None, None),
        P(),
        P(("long", "short"), None, None),
        P(),
    )
    return jax.shard_map(
        body,
        mesh=mesh,
        in_specs=placed,
        out_specs=(P(("long", "short"), None, None), P()),
        check_vma=False,
    )
```

profile of v0, /device:TPU:1, one launch (start us, length us, event | category | flops | bytes accessed | tf_op | source)
XLA Modules:
  0.0 2048.0 jit_solution(13823532065056186043)
XLA Ops:
  13.8 29.7 %custom-call.36 = f32[3,128,128]{1,2,0:T(8,128)S(1)} custom-call(f32[3,128,128]{2,1,0:T(8,128)S(1)} %get-tuple-element.384), custom_call_target="InvertDiagBlocksLowerTriangular" | custom-call | tf_op jit(solution)/shard_map/while/body/eval_jaxpr/jit(_solve_triangular)/triangular_solve | solution.py:24
  53.0 11.7 cholesky.916
  77.4 11.7 cholesky.935
  100.3 11.7 cholesky.954
  125.0 29.7 %custom-call.93 = f32[3,128,128]{1,2,0:T(8,128)S(1)} custom-call(f32[3,128,128]{2,1,0:T(8,128)S(1)} %get-tuple-element.478), custom_call_target="InvertDiagBlocksLowerTriangular" | custom-call | tf_op jit(solution)/shard_map/while/body/eval_jaxpr/jit(_solve_triangular)/triangular_solve | solution.py:28
  242.3 149.4 %conditional.6 = (f32[384,384]{1,0:T(8,128)}, f32[384,1280]{1,0:T(8,128)}, f32[384,896]{1,0:T(8,128)}, f32[384,1280]{1,0:T(8,128)}, f32[384,512]{1,0:T(8,128)}) conditional(s32[]{:T(128)} %convert_element_type.67, f32[384,384]{1,0:T(8,128)S(1)} %copy.32, (f32[384,384]{0,1:T(8,128)}, f32[384,384]{0,1:T(8,128)}, f32[384,384]{0,1:T(8,128)}, ...), branch_computations={%region_6.9_spmd, %region_7.10_spmd} | conditional | flops 6447055360 | bytes 40899376 | solution.py:77
  246.5 11.7 cholesky.598
  274.1 13.2 cholesky.617
  305.2 11.7 cholesky.636
  331.6 31.3 %custom-call.66 = f32[3,128,128]{1,2,0:T(8,128)} custom-call(f32[3,128,128]{2,1,0:T(8,128)} %get-tuple-element.465), custom_call_target="InvertDiagBlocksLowerTriangular" | custom-call | tf_op jit(solution)/shard_map/cond/branch_1_fun/jit(_solve_triangular)/triangular_solve | solution.py:24
  404.8 68.6 %collective-permute-done.4 = f32[384,896]{0,1:T(8,128)} collective-permute-done((f32[384,896]{0,1:T(8,128)}, f32[384,896]{0,1:T(8,128)}, u32[]{:S(2)}, u32[]{:S(2)}) %collective-permute-start.4) | collective-permute-done | bytes 1376288 | tf_op jit(solution)/shard_map/ppermute | solution.py:12
  480.6 26.8 %collective-permute-done.6 = f32[384,384]{0,1:T(8,128)} collective-permute-done((f32[384,384]{0,1:T(8,128)}, f32[384,384]{0,1:T(8,128)}, u32[]{:S(2)}, u32[]{:S(2)}) %collective-permute-start.6) | collective-permute-done | bytes 589856 | tf_op jit(solution)/shard_map/ppermute | solution.py:12
  507.4 15.7 conditional.7
  535.4 68.4 %collective-permute-done.7 = f32[384,896]{0,1:T(8,128)} collective-permute-done((f32[384,896]{0,1:T(8,128)}, f32[384,896]{0,1:T(8,128)}, u32[]{:S(2)}, u32[]{:S(2)}) %collective-permute-start.7) | collective-permute-done | bytes 1376288 | tf_op jit(solution)/shard_map/ppermute | solution.py:12
  610.5 11.5 collective-permute-done.9
  622.0 15.5 conditional.8
  649.0 31.8 %collective-permute-done.10 = f32[384,896]{0,1:T(8,128)} collective-permute-done((f32[384,896]{0,1:T(8,128)}, f32[384,896]{0,1:T(8,128)}, u32[]{:S(2)}, u32[]{:S(2)}) %collective-permute-start.10) | collective-permute-done | bytes 1376288 | tf_op jit(solution)/shard_map/ppermute | solution.py:12
  686.8 13.4 collective-permute-done.12
  700.3 15.7 conditional.9
  727.9 65.8 %collective-permute-done.13 = f32[384,896]{0,1:T(8,128)} collective-permute-done((f32[384,896]{0,1:T(8,128)}, f32[384,896]{0,1:T(8,128)}, u32[]{:S(2)}, u32[]{:S(2)}) %collective-permute-start.13) | collective-permute-done | bytes 1376288 | tf_op jit(solution)/shard_map/ppermute | solution.py:12
  799.8 12.3 collective-permute-done.15
  891.0 30.3 %custom-call.87 = f32[3,128,128]{1,2,0:T(8,128)} custom-call(f32[3,128,128]{2,1,0:T(8,128)S(1)} %get-tuple-element.472), custom_call_target="InvertDiagBlocksLowerTriangular" | custom-call | tf_op jit(solution)/shard_map/jit(_solve_triangular)/triangular_solve | solution.py:28
  921.3 691.3 %all-reduce.4.cloned.1.call-done = (f32[384,384]{0,1:T(8,128)}, f32[384,128]{1,0:T(8,128)}) async-done(((f32[384,384]{0,1:T(8,128)}, f32[384,128]{1,0:T(8,128)}), (f32[384,384]{0,1:T(8,128)}, f32[384,128]{1,0:T(8,128)})) %all-reduce.4.cloned.1.call-update) | async-done | bytes 786448 | tf_op jit(solution)/shard_map/psum | solution.py:225
  1616.1 11.7 cholesky.969
  1638.9 13.2 cholesky.988
  1670.3 11.7 cholesky.1007
  1696.3 29.5 %custom-call.86 = f32[3,128,128]{1,2,0:T(8,128)S(1)} custom-call(f32[3,128,128]{2,1,0:T(8,128)S(1)} %get-tuple-element.471), custom_call_target="InvertDiagBlocksLowerTriangular" | custom-call | tf_op jit(solution)/shard_map/jit(_solve_triangular)/triangular_solve | solution.py:28
  1749.9 30.1 %custom-call.88 = f32[3,128,128]{1,2,0:T(8,128)} custom-call(f32[3,128,128]{2,1,0:T(8,128)S(1)} %get-tuple-element.473), custom_call_target="InvertDiagBlocksLowerTriangular" | custom-call | tf_op jit(solution)/shard_map/jit(_solve_triangular)/triangular_solve | solution.py:28
  1805.2 30.3 %custom-call.89 = f32[3,128,128]{1,2,0:T(8,128)S(1)} custom-call(f32[3,128,128]{2,1,0:T(8,128)} %copy-done.44), custom_call_target="InvertDiagBlocksLowerTriangular" | custom-call | tf_op jit(solution)/shard_map/jit(_solve_triangular)/triangular_solve | solution.py:28
  1864.4 30.1 %custom-call.90 = f32[3,128,128]{1,2,0:T(8,128)} custom-call(f32[3,128,128]{2,1,0:T(8,128)S(1)} %get-tuple-element.475), custom_call_target="InvertDiagBlocksLowerTriangular" | custom-call | tf_op jit(solution)/shard_map/jit(_solve_triangular)/triangular_solve | solution.py:28
  1920.5 30.3 %custom-call.91 = f32[3,128,128]{1,2,0:T(8,128)S(1)} custom-call(f32[3,128,128]{2,1,0:T(8,128)} %copy-done.45), custom_call_target="InvertDiagBlocksLowerTriangular" | custom-call | tf_op jit(solution)/shard_map/jit(_solve_triangular)/triangular_solve | solution.py:28
  1981.3 30.1 %custom-call.92 = f32[3,128,128]{1,2,0:T(8,128)} custom-call(f32[3,128,128]{2,1,0:T(8,128)S(1)} %get-tuple-element.477), custom_call_target="InvertDiagBlocksLowerTriangular" | custom-call | tf_op jit(solution)/shard_map/jit(_solve_triangular)/triangular_solve | solution.py:28
  (512 shorter events, 690.6 us)
Async XLA Ops:
  7.2 1605.4 %all-reduce.4.cloned.1.call-start = ((), (), s32[]{:S(2)}) async-start(), calls=%async_computation | async-start | bytes 1572864 | tf_op jit(solution)/shard_map/psum | solution.py:225
  195.4 35.3 %collective-permute-start.2 = (f32[384,384]{0,1:T(8,128)}, f32[384,384]{0,1:T(8,128)}, u32[]{:S(2)}, u32[]{:S(2)}) collective-permute-start(f32[384,384]{0,1:T(8,128)} %fusion.208), channel_id=1, source_target_pairs={{1,0},{2,1},{3,2},{4,3},{5,4},{6,5},{7,6},{8,7},{9,8},{10,9},{11,1... | collective-permute-start | bytes 1769480 | tf_op jit(solution)/shard_map/ppermute | solution.py:12
  205.3 27.7 %collective-permute-start = (f32[384,384]{0,1:T(8,128)}, f32[384,384]{0,1:T(8,128)}, u32[]{:S(2)}, u32[]{:S(2)}) collective-permute-start(f32[384,384]{0,1:T(8,128)} %fusion.210), channel_id=1, source_target_pairs={{1,0},{2,1},{3,2},{4,3},{5,4},{6,5},{7,6},{8,7},{9,8},{10,9},{11,1... | collective-permute-start | bytes 1769480 | tf_op jit(solution)/shard_map/ppermute | solution.py:12
  210.4 19.3 collective-permute-start.3
  215.1 27.2 %collective-permute-start.1 = (f32[384,384]{0,1:T(8,128)}, f32[384,384]{0,1:T(8,128)}, u32[]{:S(2)}, u32[]{:S(2)}) collective-permute-start(f32[384,384]{0,1:T(8,128)} %neg.42), channel_id=1, source_target_pairs={{1,0},{2,1},{3,2},{4,3},{5,4},{6,5},{7,6},{8,7},{9,8},{10,9},{11,1... | collective-permute-start | bytes 1769480 | tf_op jit(solution)/shard_map/ppermute | solution.py:12
  394.5 78.8 %collective-permute-start.5 = (f32[384,1280]{0,1:T(8,128)}, f32[384,1280]{0,1:T(8,128)}, u32[]{:S(2)}, u32[]{:S(2)}) collective-permute-start(f32[384,1280]{0,1:T(8,128)} %copy.35), channel_id=1, source_target_pairs={{0,1},{1,2},{2,3},{3,4},{4,5},{5,6},{6,7},{7,8},{8,9},{9,10},{10,1... | collective-permute-start | bytes 5898248 | tf_op jit(solution)/shard_map/ppermute | solution.py:12
  399.3 74.0 %collective-permute-start.4 = (f32[384,896]{0,1:T(8,128)}, f32[384,896]{0,1:T(8,128)}, u32[]{:S(2)}, u32[]{:S(2)}) collective-permute-start(f32[384,896]{0,1:T(8,128)} %copy.34), channel_id=1, source_target_pairs={{1,0},{2,1},{3,2},{4,3},{5,4},{6,5},{7,6},{8,7},{9,8},{10,9},{11,1... | collective-permute-start | bytes 4128776 | tf_op jit(solution)/shard_map/ppermute | solution.py:12
  477.0 30.5 %collective-permute-start.6 = (f32[384,384]{0,1:T(8,128)}, f32[384,384]{0,1:T(8,128)}, u32[]{:S(2)}, u32[]{:S(2)}) collective-permute-start(f32[384,384]{0,1:T(8,128)} %get-tuple-element.767), channel_id=1, source_target_pairs={{2,0},{3,1},{4,2},{5,3},{6,4},{7,5},{8,6},{9,7},{10,8},{11,9},{12,... | collective-permute-start | bytes 1769480 | tf_op jit(solution)/shard_map/ppermute | solution.py:12
  526.0 77.7 %collective-permute-start.8 = (f32[384,1280]{0,1:T(8,128)}, f32[384,1280]{0,1:T(8,128)}, u32[]{:S(2)}, u32[]{:S(2)}) collective-permute-start(f32[384,1280]{0,1:T(8,128)} %copy.39), channel_id=1, source_target_pairs={{0,2},{1,3},{2,4},{3,5},{4,6},{5,7},{6,8},{7,9},{8,10},{9,11},{10,... | collective-permute-start | bytes 5898248 | tf_op jit(solution)/shard_map/ppermute | solution.py:12
  530.8 72.9 %collective-permute-start.7 = (f32[384,896]{0,1:T(8,128)}, f32[384,896]{0,1:T(8,128)}, u32[]{:S(2)}, u32[]{:S(2)}) collective-permute-start(f32[384,896]{0,1:T(8,128)} %copy.38), channel_id=1, source_target_pairs={{2,0},{3,1},{4,2},{5,3},{6,4},{7,5},{8,6},{9,7},{10,8},{11,9},{12,... | collective-permute-start | bytes 4128776 | tf_op jit(solution)/shard_map/ppermute | solution.py:12
  607.4 14.6 collective-permute-start.9
  640.4 40.3 %collective-permute-start.11 = (f32[384,1280]{0,1:T(8,128)}, f32[384,1280]{0,1:T(8,128)}, u32[]{:S(2)}, u32[]{:S(2)}) collective-permute-start(f32[384,1280]{0,1:T(8,128)} %copy.43), channel_id=1, source_target_pairs={{0,4},{4,8},{8,12},{12,16},{16,20},{20,24},{24,28},{1,5},{5,9},{9,... | collective-permute-start | bytes 5898248 | tf_op jit(solution)/shard_map/ppermute | solution.py:12
  645.2 35.5 %collective-permute-start.10 = (f32[384,896]{0,1:T(8,128)}, f32[384,896]{0,1:T(8,128)}, u32[]{:S(2)}, u32[]{:S(2)}) collective-permute-start(f32[384,896]{0,1:T(8,128)} %copy.42), channel_id=1, source_target_pairs={{4,0},{8,4},{12,8},{16,12},{20,16},{24,20},{28,24},{5,1},{9,5},{13... | collective-permute-start | bytes 4128776 | tf_op jit(solution)/shard_map/ppermute | solution.py:12
  684.4 15.9 collective-permute-start.12
  718.9 74.8 %collective-permute-start.14 = (f32[384,1280]{0,1:T(8,128)}, f32[384,1280]{0,1:T(8,128)}, u32[]{:S(2)}, u32[]{:S(2)}) collective-permute-start(f32[384,1280]{0,1:T(8,128)} %copy.47), channel_id=1, source_target_pairs={{0,8},{4,12},{8,16},{12,20},{16,24},{20,28},{1,9},{5,13},{9,17},{1... | collective-permute-start | bytes 5898248 | tf_op jit(solution)/shard_map/ppermute | solution.py:12
  726.5 67.1 %collective-permute-start.13 = (f32[384,896]{0,1:T(8,128)}, f32[384,896]{0,1:T(8,128)}, u32[]{:S(2)}, u32[]{:S(2)}) collective-permute-start(f32[384,896]{0,1:T(8,128)} %copy.46), channel_id=1, source_target_pairs={{8,0},{12,4},{16,8},{20,12},{24,16},{28,20},{9,1},{13,5},{17,9},{2... | collective-permute-start | bytes 4128776 | tf_op jit(solution)/shard_map/ppermute | solution.py:12
  797.3 14.8 collective-permute-start.15
  823.4 40.7 %collective-permute-start.17 = (f32[384,1280]{0,1:T(8,128)}, f32[384,1280]{0,1:T(8,128)}, u32[]{:S(2)}, u32[]{:S(2)}) collective-permute-start(f32[384,1280]{0,1:T(8,128)} %copy.51), channel_id=1, source_target_pairs={{0,16},{4,20},{8,24},{12,28},{1,17},{5,21},{9,25},{13,29},{2,18},{... | collective-permute-start | bytes 5898248 | tf_op jit(solution)/shard_map/ppermute | solution.py:12
  828.9 30.6 %collective-permute-start.16 = (f32[384,896]{0,1:T(8,128)}, f32[384,896]{0,1:T(8,128)}, u32[]{:S(2)}, u32[]{:S(2)}) collective-permute-start(f32[384,896]{0,1:T(8,128)} %copy.50), channel_id=1, source_target_pairs={{16,0},{20,4},{24,8},{28,12},{17,1},{21,5},{25,9},{29,13},{18,2},{... | collective-permute-start | bytes 4128776 | tf_op jit(solution)/shard_map/ppermute | solution.py:12
  876.6 736.0 %copy-start.53 = (f32[384]{0:T(512)S(1)}, f32[384]{0:T(512)}, u32[]{:S(2)}) copy-start(f32[384]{0:T(512)} %param.28) | copy-start | bytes 4612
  1733.0 303.4 %copy-start.4 = (f32[384,128]{1,0:T(8,128)}, f32[384,128]{1,0:T(8,128)S(1)}, u32[]{:S(2)}) copy-start(f32[384,128]{1,0:T(8,128)S(1)} %pad_maximum_fusion.17) | copy-start | bytes 589828
  1737.9 43.5 %collective-permute-start.18 = (f32[384,128]{1,0:T(8,128)S(1)}, f32[384,128]{1,0:T(8,128)S(1)}, u32[]{:S(2)}, u32[]{:S(2)}) collective-permute-start(f32[384,128]{1,0:T(8,128)S(1)} %maximum_select_fusion), channel_id=1, source_target_pairs={{0,16},{4,20},{8,24},{12,28},{1,17},{5,21},{9,25},{13,29},{2,18},{... | collective-permute-start | bytes 589832 | tf_op jit(solution)/shard_map/ppermute | solution.py:12
  1780.0 6.5 collective-permute-start.19
  1793.1 43.7 %collective-permute-start.20 = (f32[384,128]{1,0:T(8,128)S(1)}, f32[384,128]{1,0:T(8,128)}, u32[]{:S(2)}, u32[]{:S(2)}) collective-permute-start(f32[384,128]{1,0:T(8,128)S(1)} %maximum_select_fusion.1), channel_id=1, source_target_pairs={{0,8},{4,12},{8,16},{12,20},{16,24},{20,28},{1,9},{5,13},{9,17},{1... | collective-permute-start | bytes 589832 | tf_op jit(solution)/shard_map/ppermute | solution.py:12
  1835.5 6.4 collective-permute-start.21
  1848.5 48.0 %collective-permute-start.22 = (f32[384,128]{1,0:T(8,128)S(1)}, f32[384,128]{1,0:T(8,128)S(1)}, u32[]{:S(2)}, u32[]{:S(2)}) collective-permute-start(f32[384,128]{1,0:T(8,128)S(1)} %maximum_select_fusion.2), channel_id=1, source_target_pairs={{0,4},{4,8},{8,12},{12,16},{16,20},{20,24},{24,28},{1,5},{5,9},{9,... | collective-permute-start | bytes 589832 | tf_op jit(solution)/shard_map/ppermute | solution.py:12
  1894.5 7.1 collective-permute-start.23
  1908.2 46.1 %collective-permute-start.24 = (f32[384,128]{1,0:T(8,128)S(1)}, f32[384,128]{1,0:T(8,128)}, u32[]{:S(2)}, u32[]{:S(2)}) collective-permute-start(f32[384,128]{1,0:T(8,128)S(1)} %maximum_select_fusion.3), channel_id=1, source_target_pairs={{0,2},{1,3},{2,4},{3,5},{4,6},{5,7},{6,8},{7,9},{8,10},{9,11},{10,... | collective-permute-start | bytes 589832 | tf_op jit(solution)/shard_map/ppermute | solution.py:12
  1950.8 13.1 collective-permute-start.25
  1970.5 46.5 %collective-permute-start.26 = (f32[384,128]{1,0:T(8,128)S(1)}, f32[384,128]{1,0:T(8,128)S(1)}, u32[]{:S(2)}, u32[]{:S(2)}) collective-permute-start(f32[384,128]{1,0:T(8,128)S(1)} %maximum_select_fusion.4), channel_id=1, source_target_pairs={{0,1},{1,2},{2,3},{3,4},{4,5},{5,6},{6,7},{7,8},{8,9},{9,10},{10,1... | collective-permute-start | bytes 589832 | tf_op jit(solution)/shard_map/ppermute | solution.py:12
  2011.4 8.9 collective-permute-start.27
  2027.0 8.8 collective-permute-start.28
  (40 other events, 496.2 us)
Sparse Core Ops, SparseCore 0:
  882.2 730.3 all-reduce.3
where the time goes:
time: 2060 us; the launch traced here: 2050 us
  waiting for transfers between devices  1040 us (50%)
  other arithmetic  542 us (26%)
  local copies, waits for them, and re-layouts  197 us (10%)
  matrix products  129 us (6%)
  starting transfers between devices  82.9 us (4%)
  loops' own time  39.9 us (2%)
    psum x1, waiting for transfers between devices, body(): lax.psum((tip_terms, tip_rhs_terms), ('long', 'short'))  691 us
    ppermute x29, waiting for transfers between devices, shifted(): return lax.ppermute(block, axis, route)  346 us
    another operation x17, other arithmetic, solve_upper(): jax.scipy.linalg.solve_triangular(factor, values, lower=True, trans=1)  253 us
    ppermute x29, starting transfers between devices, shifted(): return lax.ppermute(block, axis, route)  82.8 us
    another operation x78, local copies, waits for them, and re-layouts, solve_upper(): jax.scipy.linalg.solve_triangular(factor, values, lower=True, trans=1)  69.3 us
    another operation x9, other arithmetic, solve_lower(): return jax.scipy.linalg.solve_triangular(factor, values, lower=True)  64.7 us
    another operation x10, other arithmetic, eliminate(): factor = jnp.linalg.cholesky(diag_item)  62.8 us
    another operation x11, other arithmetic, body(): tip_factor = jnp.linalg.cholesky(tip_total + jnp.diag(prior))  61 us
  transfers between devices with their start and end apart: 30, of which 19 were waited for; matrix products, arithmetic and copies ran while one was open for 15% of the time, Pallas kernels for 0%

commit v1 on v0

v1 whole, which is shorter than its diff:
```python
import jax
import jax.numpy as jnp
from jax import lax
from jax.experimental import pallas as pl
from jax.experimental.pallas import tpu as pltpu
from jax.sharding import PartitionSpec as P

AXES = ("long", "short")
PREC = lax.Precision.HIGHEST
LANES = 128
SUBLANES = 8


def gram_prod(left, right):
    return jnp.einsum("ji,jk->ik", left, right, precision=PREC)


def mat_prod(left, right):
    return jnp.matmul(left, right, precision=PREC)


def pivot_pair(tiles, first, lane, sub):
    group, row = divmod(first, SUBLANES)
    shape = (SUBLANES, LANES)
    col0 = [jnp.broadcast_to(t[:, first : first + 1], shape) for t in tiles]
    col1 = [jnp.broadcast_to(t[:, first + 1 : first + 2], shape) for t in tiles]
    at0, at1 = lane == first, lane == first + 1
    a = col0[group][row : row + 1, :]
    b = col1[group][row : row + 1, :]
    c = col1[group][row + 1 : row + 2, :]
    inv = 1.0 / (a * c - b * b)
    row0 = tiles[group][row : row + 1, :]
    row1 = tiles[group][row + 1 : row + 2, :]
    at0_row, at1_row = at0[:1], at1[:1]
    row0 = jnp.where(at0_row, 1.0, jnp.where(at1_row, 0.0, row0))
    row1 = jnp.where(at1_row, 1.0, jnp.where(at0_row, 0.0, row1))
    q0 = jnp.broadcast_to((c * row0 - b * row1) * inv, shape)
    q1 = jnp.broadcast_to((a * row1 - b * row0) * inv, shape)
    both = jnp.logical_or(at0, at1)
    out = []
    for place, tile in enumerate(tiles):
        new = jnp.where(both, 0.0, tile) - col0[place] * q0 - col1[place] * q1
        if place == group:
            new = jnp.where(sub == row, q0, jnp.where(sub == row + 1, q1, new))
        out.append(new)
    return out


def inverse_kernel(a_ref, o_ref):
    width = a_ref.shape[0]
    lane = lax.broadcasted_iota(jnp.int32, (SUBLANES, LANES), 1)
    sub = lax.broadcasted_iota(jnp.int32, (SUBLANES, LANES), 0)
    o_ref[...] = a_ref[...]

    def step(k, carry):
        at = pl.multiple_of(k * LANES, LANES)
        here = pl.ds(at, LANES)
        tiles = [
            o_ref[pl.ds(pl.multiple_of(at + SUBLANES * g, SUBLANES), SUBLANES), here]
            for g in range(LANES // SUBLANES)
        ]
        for first in range(0, LANES, 2):
            tiles = pivot_pair(tiles, first, lane, sub)
        pivot = jnp.concatenate(tiles, axis=0)
        rows = o_ref[here, :]
        columns = o_ref[:, here]
        scaled = jnp.dot(pivot, rows, precision=PREC, preferred_element_type=jnp.float32)
        o_ref[here, :] = scaled
        o_ref[here, here] = pivot
        scaled = o_ref[here, :]
        o_ref[:, here] = jnp.zeros((width, LANES), jnp.float32)
        o_ref[...] = o_ref[...] - jnp.dot(
            columns, scaled, precision=PREC, preferred_element_type=jnp.float32
        )
        o_ref[here, :] = scaled
        return carry

    lax.fori_loop(0, width // LANES, step, 0)


def spd_inverse(matrix):
    width = matrix.shape[0]
    return pl.pallas_call(
        inverse_kernel,
        out_shape=jax.ShapeDtypeStruct(matrix.shape, jnp.float32),
        in_specs=[pl.BlockSpec(memory_space=pltpu.VMEM)],
        out_specs=pl.BlockSpec(memory_space=pltpu.VMEM),
        cost_estimate=pl.CostEstimate(
            flops=300 * width**3, bytes_accessed=8 * width**2, transcendentals=0
        ),
        name="spd_inverse",
    )(matrix)


def body(transition, innovation, observation, effects, prior, right_side, tip_right):
    block_count, node_width = innovation.shape
    tip_width = prior.shape[0]
    total = lax.axis_size(AXES)
    position = lax.axis_index(AXES)
    identity = jnp.eye(node_width, dtype=jnp.float32)

    def send(values, pairs):
        return lax.ppermute(values, AXES, pairs)

    weighted_trans = innovation[:, :, None] * transition
    weighted_effect = innovation[:, :, None] * effects
    succ_diag = [gram_prod(transition[t], weighted_trans[t]) for t in range(block_count)]
    succ_arrow = [gram_prod(transition[t], weighted_effect[t]) for t in range(block_count)]
    tip_terms = gram_prod(
        effects.reshape(-1, tip_width), weighted_effect.reshape(-1, tip_width)
    )
    global_block = position * block_count + jnp.arange(block_count)
    couple = -weighted_trans * jnp.where(global_block == 0, 0.0, 1.0)[:, None, None]
    diag_base = (innovation + observation)[:, :, None] * identity
    interior = block_count - 1

    stored = []
    left_diag = left_arrow = left_rhs = 0.0
    diag_item = arrow_item = rhs_item = left_item = None
    for t in range(block_count):
        if t == 0:
            diag_item = diag_base[t]
            arrow_item = -weighted_effect[t]
            rhs_item = right_side[t]
            left_item = couple[t]
        else:
            _, link, y_left, y_arrow, y_rhs = stored[-1]
            diag_item = diag_base[t] - mat_prod(couple[t], link)
            arrow_item = -weighted_effect[t] - mat_prod(couple[t], y_arrow)
            rhs_item = right_side[t] - mat_prod(couple[t], y_rhs)
            left_item = -mat_prod(couple[t], y_left)
        if t < interior:
            diag_item = diag_item + succ_diag[t + 1]
            arrow_item = arrow_item + succ_arrow[t + 1]
            inverse = spd_inverse(diag_item)
            link = jnp.einsum("ij,kj->ik", inverse, couple[t + 1], precision=PREC)
            y_left = mat_prod(inverse, left_item)
            y_arrow = mat_prod(inverse, arrow_item)
            y_rhs = mat_prod(inverse, rhs_item)
            left_diag = left_diag - gram_prod(left_item, y_left)
            left_arrow = left_arrow - gram_prod(left_item, y_arrow)
            left_rhs = left_rhs - gram_prod(left_item, y_rhs)
            tip_terms = tip_terms - gram_prod(arrow_item, y_arrow)
            tip_part = gram_prod(arrow_item, y_rhs)
            tip_rhs_terms = -tip_part if t == 0 else tip_rhs_terms - tip_part
            stored.append((inverse, link, y_left, y_arrow, y_rhs))
    if interior == 0:
        tip_rhs_terms = jnp.zeros_like(tip_right)

    to_left = [(i, i - 1) for i in range(1, total)]
    node_diag = diag_item + send(left_diag + succ_diag[0], to_left)
    node_arrow = arrow_item + send(left_arrow + succ_arrow[0], to_left)
    node_rhs = rhs_item
    if interior > 0:
        node_rhs = node_rhs + send(left_rhs, to_left)
    node_couple = left_item

    levels = []
    distance = 1
    while distance < total:
        d = distance
        drops = [i for i in range(total) if (i + 1) % d == 0 and (i + 1) // d % 2 == 1]
        rightward = [(i, i + d) for i in drops if i + d < total]
        leftward = [(i, i - d) for i in drops if i >= d]
        back_right = [(j, i) for i, j in rightward]
        back_left = [(j, i) for i, j in leftward]
        rank = position + 1
        drop = jnp.logical_and(rank % d == 0, rank // d % 2 == 1)
        fed = jnp.logical_and(rank % (2 * d) == 0, position >= d)
        right_item = send(node_couple, back_right).T
        inverse = spd_inverse(node_diag)
        y_right = mat_prod(inverse, right_item)
        y_left = mat_prod(inverse, node_couple)
        diag_right = send(gram_prod(right_item, y_right), rightward)
        diag_left = send(gram_prod(node_couple, y_left), leftward)
        y_arrow = mat_prod(inverse, node_arrow)
        y_rhs = mat_prod(inverse, node_rhs)
        new_couple = send(gram_prod(right_item, y_left), rightward)
        arrow_right = send(gram_prod(right_item, y_arrow), rightward)
        arrow_left = send(gram_prod(node_couple, y_arrow), leftward)
        rhs_right = send(gram_prod(right_item, y_rhs), rightward)
        rhs_left = send(gram_prod(node_couple, y_rhs), leftward)
        tip_terms = tip_terms - jnp.where(drop, gram_prod(node_arrow, y_arrow), 0.0)
        tip_rhs_terms = tip_rhs_terms - jnp.where(drop, gram_prod(node_arrow, y_rhs), 0.0)
        levels.append((drop, back_left, back_right, y_left, y_right, y_arrow, y_rhs))
        node_diag = node_diag - diag_right - diag_left
        node_couple = jnp.where(fed, -new_couple, node_couple)
        node_arrow = node_arrow - arrow_right - arrow_left
        node_rhs = node_rhs - rhs_right - rhs_left
        distance *= 2

    final = position == total - 1
    inverse = spd_inverse(node_diag)
    y_arrow = mat_prod(inverse, node_arrow)
    y_rhs = mat_prod(inverse, node_rhs)
    tip_terms = tip_terms - jnp.where(final, gram_prod(node_arrow, y_arrow), 0.0)
    tip_rhs_terms = tip_rhs_terms - jnp.where(final, gram_prod(node_arrow, y_rhs), 0.0)
    tip_total, tip_rhs_total = lax.psum((tip_terms, tip_rhs_terms), AXES)
    tip_solution = mat_prod(spd_inverse(tip_total + jnp.diag(prior)), tip_rhs_total + tip_right)

    node_x = y_rhs - mat_prod(y_arrow, tip_solution)
    for drop, back_left, back_right, y_left, y_right, y_arrow, y_rhs in reversed(levels):
        base = y_rhs - mat_prod(y_arrow, tip_solution)
        left_x = send(node_x, back_left)
        right_x = send(node_x, back_right)
        value = base - mat_prod(y_left, left_x) - mat_prod(y_right, right_x)
        node_x = jnp.where(drop, value, node_x)
    left_x = send(node_x, [(i, i + 1) for i in range(total - 1)])
    outs = [node_x]
    for inverse, link, y_left, y_arrow, y_rhs in reversed(stored):
        value = (
            y_rhs
            - mat_prod(y_arrow, tip_solution)
            - mat_prod(y_left, left_x)
            - mat_prod(link, outs[0])
        )
        outs.insert(0, value)
    return (jnp.stack(outs, axis=0), tip_solution)


def solution(mesh):
    placed = (
        P(AXES, None, None),
        P(AXES, None),
        P(AXES, None),
        P(AXES, None, None),
        P(),
        P(AXES, None, None),
        P(),
    )
    return jax.shard_map(
        body,
        mesh=mesh,
        in_specs=placed,
        out_specs=(P(AXES, None, None), P()),
        check_vma=False,
    )
```

time: 2060 us -> 763 us (0.37)
  waiting for transfers between devices: 1040 us -> 229 us
  other arithmetic: 542 us -> 22.5 us
  Pallas kernels: 0 us -> 226 us
  local copies, waits for them, and re-layouts: 197 us -> 2.61 us
  loops' own time: 39.9 us -> 0 us
  matrix products: 129 us -> 164 us
    psum x1, waiting for transfers between devices: 691 us -> 175 us  [body(): tip_total, tip_rhs_total = lax.psum((tip_terms, tip_rhs_terms), AXES)]
    another operation x57 -> x1, other arithmetic: 497 us -> 0.77 us  [body(): return (jnp.stack(outs, axis=0), tip_solution)]
    ppermute x29 -> x53, waiting for transfers between devices: 346 us -> 53.6 us  [send(): return lax.ppermute(values, AXES, pairs)]
    pallas_call x0 -> x8, Pallas kernels: none -> 226 us  [spd_inverse(): pl.pallas_call(inverse_kernel, out_shape=jax.ShapeDtypeStruct(matrix.shap...]
    another operation x140 -> x0, local copies, waits for them, and re-layouts: 119 us -> none  [the longest x78 69.3 us: solve_upper(): jax.scipy.linalg.solve_triangular(factor, values, lower=True, trans=1)]
    dot_general x28 -> x106, matrix products: 72.4 us -> 164 us  [the longest x56 101 us: gram_prod(): return jnp.einsum('ji,jk->ik', left, right, precision=PREC)]
    another operation x72 -> x0, matrix products: 56.7 us -> none  [the longest x40 24 us: solve_upper(): jax.scipy.linalg.solve_triangular(factor, values, lower=True, trans=1)]
    cond x24 -> x0, local copies, waits for them, and re-layouts: 46.6 us -> none  [the longest x15 40.2 us: reduce_level(): lax.cond(drop, eliminate, skip, (node_diag, node_couple, right_couple, no...]
  transfers between devices with their start and end apart: 30 -> 54, of which waited for: 19 -> 6; matrix products, arithmetic and copies ran while one was open for 15% -> 21% of each run, Pallas kernels for 0% -> 22%
where the time goes in v1:
time: 763 us; the launch traced here: 755 us
  waiting for transfers between devices  229 us (30%)
  Pallas kernels  226 us (30%)
  matrix products  164 us (21%)
  starting transfers between devices  94.7 us (12%)
  other arithmetic  22.5 us (3%)
  between operations  16.6 us (2%)
    pallas_call x8, Pallas kernels, spd_inverse(): pl.pallas_call(inverse_kernel, out_shape=jax.ShapeDtypeStruct(matrix.shap...  226 us
    psum x1, waiting for transfers between devices, body(): tip_total, tip_rhs_total = lax.psum((tip_terms, tip_rhs_terms), AXES)  175 us
    dot_general x56, matrix products, gram_prod(): return jnp.einsum('ji,jk->ik', left, right, precision=PREC)  101 us
    ppermute x53, starting transfers between devices, send(): return lax.ppermute(values, AXES, pairs)  94.6 us
    dot_general x49, matrix products, mat_prod(): return jnp.matmul(left, right, precision=PREC)  61.6 us
    ppermute x53, waiting for transfers between devices, send(): return lax.ppermute(values, AXES, pairs)  53.6 us
  transfers between devices with their start and end apart: 54, of which 6 were waited for; matrix products, arithmetic and copies ran while one was open for 21% of the time, Pallas kernels for 22%

profile of v1, /device:TPU:1, one launch (start us, length us, event | category | flops | bytes accessed | tf_op | source)
XLA Modules:
  0.0 755.0 jit_solution(6852494486792200217)
XLA Ops:
  14.6 28.1 %spd_inverse.8 = f32[384,384]{1,0:T(8,128)} custom-call(f32[384,384]{1,0:T(8,128)} %fusion.9.a_ref), custom_call_target="tpu_custom_call" | custom-call | flops 16986931200 | bytes 1179648 | tf_op jit(solution)/shard_map/spd_inverse/pallas_call | solution.py:83
  46.3 8.5 %collective-permute-start.31 = (f32[384,128]{1,0:T(8,128)}, f32[384,128]{1,0:T(8,128)}, u32[]{:S(2)}, u32[]{:S(2)}) collective-permute-start(f32[384,128]{1,0:T(8,128)} %convolution_subtract_fusion.13), channel_id=1, source_target_pairs={{1,0},{2,1},{3,2},{4,3},{5,4},{6,5},{7,6},{8,7},{9,8},{10,9},{11,1... | collective-permute-start | bytes 589832 | tf_op jit(solution)/shard_map/ppermute | solution.py:103
  56.2 2.6 convolution_bitcast_fusion.1
  62.2 7.4 collective-permute-start
  77.0 8.5 %collective-permute-start.1 = (f32[384,384]{1,0:T(8,128)}, f32[384,384]{1,0:T(8,128)}, u32[]{:S(2)}, u32[]{:S(2)}) collective-permute-start(f32[384,384]{1,0:T(8,128)} %fusion.7), channel_id=1, source_target_pairs={{1,0},{2,1},{3,2},{4,3},{5,4},{6,5},{7,6},{8,7},{9,8},{10,9},{11,1... | collective-permute-start | bytes 1769480 | tf_op jit(solution)/shard_map/ppermute | solution.py:103
  85.6 2.4 convolution_bitcast_fusion.2
  93.3 16.5 %collective-permute-done.1 = f32[384,384]{1,0:T(8,128)} collective-permute-done((f32[384,384]{1,0:T(8,128)}, f32[384,384]{1,0:T(8,128)}, u32[]{:S(2)}, u32[]{:S(2)}) %collective-permute-start.1) | collective-permute-done | bytes 589856 | tf_op jit(solution)/shard_map/ppermute | solution.py:103
  109.8 3.2 fusion.6.a_ref
  113.0 28.3 %spd_inverse.9 = f32[384,384]{1,0:T(8,128)} custom-call(f32[384,384]{1,0:T(8,128)} %fusion.6.a_ref), custom_call_target="tpu_custom_call" | custom-call | flops 16986931200 | bytes 1179648 | tf_op jit(solution)/shard_map/spd_inverse/pallas_call | solution.py:83
  144.5 2.6 fusion.4
  153.1 3.9 collective-permute-start.6
  168.5 4.7 collective-permute-start.32
  173.2 4.7 collective-permute-start.33
  180.1 3.5 collective-permute-start.4
  185.7 5.0 collective-permute-done.5
  192.3 28.2 %spd_inverse.10 = f32[384,384]{1,0:T(8,128)} custom-call(f32[384,384]{1,0:T(8,128)} %subtract_subtract_fusion.9.a_ref), custom_call_target="tpu_custom_call" | custom-call | flops 16986931200 | bytes 1179648 | tf_op jit(solution)/shard_map/spd_inverse/pallas_call | solution.py:83
  250.8 28.1 %spd_inverse.11 = f32[384,384]{1,0:T(8,128)} custom-call(f32[384,384]{1,0:T(8,128)} %subtract_subtract_fusion.7.a_ref), custom_call_target="tpu_custom_call" | custom-call | flops 16986931200 | bytes 1179648 | tf_op jit(solution)/shard_map/spd_inverse/pallas_call | solution.py:83
  312.4 28.2 %spd_inverse.12 = f32[384,384]{1,0:T(8,128)} custom-call(f32[384,384]{1,0:T(8,128)} %subtract_subtract_fusion.5.a_ref), custom_call_target="tpu_custom_call" | custom-call | flops 16986931200 | bytes 1179648 | tf_op jit(solution)/shard_map/spd_inverse/pallas_call | solution.py:83
  366.1 2.5 fusion.69
  369.5 3.1 fusion.66
  380.2 28.2 %spd_inverse.13 = f32[384,384]{1,0:T(8,128)} custom-call(f32[384,384]{1,0:T(8,128)} %subtract_subtract_fusion.3.a_ref), custom_call_target="tpu_custom_call" | custom-call | flops 16986931200 | bytes 1179648 | tf_op jit(solution)/shard_map/spd_inverse/pallas_call | solution.py:83
  410.2 2.4 fusion.78
  426.4 2.5 fusion.77
  434.4 2.4 fusion.92
  438.1 3.1 fusion.74
  443.9 28.2 %spd_inverse.14 = f32[384,384]{1,0:T(8,128)} custom-call(f32[384,384]{1,0:T(8,128)} %subtract_subtract_fusion.a_ref), custom_call_target="tpu_custom_call" | custom-call | flops 16986931200 | bytes 1179648 | tf_op jit(solution)/shard_map/spd_inverse/pallas_call | solution.py:83
  482.5 175.2 %all-reduce.3.cloned.1.call-done = (f32[384,384]{1,0:T(8,128)}, f32[384,128]{1,0:T(8,128)}) async-done(((f32[384,384]{1,0:T(8,128)}, f32[384,128]{1,0:T(8,128)}), (f32[384,384]{1,0:T(8,128)}, f32[384,128]{1,0:T(8,128)})) %all-reduce.3.cloned.1.call-update) | async-done | bytes 786448 | tf_op jit(solution)/shard_map/psum | solution.py:198
  659.7 28.3 %spd_inverse.15 = f32[384,384]{1,0:T(8,128)} custom-call(f32[384,384]{1,0:T(8,128)} %select_add_fusion.a_ref), custom_call_target="tpu_custom_call" | custom-call | flops 16986931200 | bytes 1179648 | tf_op jit(solution)/shard_map/spd_inverse/pallas_call | solution.py:83
  709.6 21.9 %collective-permute-done.50 = f32[384,128]{1,0:T(8,128)S(1)} collective-permute-done((f32[384,128]{1,0:T(8,128)S(1)}, f32[384,128]{1,0:T(8,128)S(1)}, u32[]{:S(2)}, u32[]{:S(2)}) %collective-permute-start.50) | collective-permute-done | bytes 196640 | tf_op jit(solution)/shard_map/ppermute | solution.py:103
  732.2 2.4 collective-permute-done.51
  735.2 2.7 collective-permute-start.52
  738.6 7.7 %collective-permute-done.52 = f32[384,128]{1,0:T(8,128)S(1)} collective-permute-done((f32[384,128]{1,0:T(8,128)S(1)}, f32[384,128]{1,0:T(8,128)S(1)}, u32[]{:S(2)}, u32[]{:S(2)}) %collective-permute-start.52) | collective-permute-done | bytes 196640 | tf_op jit(solution)/shard_map/ppermute | solution.py:103
  (401 shorter events, 213.4 us)
Async XLA Ops:
  7.2 650.5 %all-reduce.3.cloned.1.call-start = ((), (), s32[]{:S(2)}) async-start(), calls=%async_computation | async-start | bytes 1572864 | tf_op jit(solution)/shard_map/psum | solution.py:198
  46.3 45.1 %collective-permute-start.31 = (f32[384,128]{1,0:T(8,128)}, f32[384,128]{1,0:T(8,128)}, u32[]{:S(2)}, u32[]{:S(2)}) collective-permute-start(f32[384,128]{1,0:T(8,128)} %convolution_subtract_fusion.13), channel_id=1, source_target_pairs={{1,0},{2,1},{3,2},{4,3},{5,4},{6,5},{7,6},{8,7},{9,8},{10,9},{11,1... | collective-permute-start | bytes 589832 | tf_op jit(solution)/shard_map/ppermute | solution.py:103
  62.2 82.3 %collective-permute-start = (f32[384,384]{1,0:T(8,128)}, f32[384,384]{1,0:T(8,128)}, u32[]{:S(2)}, u32[]{:S(2)}) collective-permute-start(f32[384,384]{1,0:T(8,128)} %fusion.5), channel_id=1, source_target_pairs={{1,0},{2,1},{3,2},{4,3},{5,4},{6,5},{7,6},{8,7},{9,8},{10,9},{11,1... | collective-permute-start | bytes 1769480 | tf_op jit(solution)/shard_map/ppermute | solution.py:103
  72.1 88.3 %collective-permute-start.2 = (f32[384,384]{1,0:T(8,128)S(1)}, f32[384,384]{1,0:T(8,128)S(1)}, u32[]{:S(2)}, u32[]{:S(2)}) collective-permute-start(f32[384,384]{1,0:T(8,128)S(1)} %convolution_negate_fusion), channel_id=1, source_target_pairs={{1,0},{3,2},{5,4},{7,6},{9,8},{11,10},{13,12},{15,14},{17,16},{19,... | collective-permute-start | bytes 1769480 | tf_op jit(solution)/shard_map/ppermute | solution.py:103
  77.0 32.8 %collective-permute-start.1 = (f32[384,384]{1,0:T(8,128)}, f32[384,384]{1,0:T(8,128)}, u32[]{:S(2)}, u32[]{:S(2)}) collective-permute-start(f32[384,384]{1,0:T(8,128)} %fusion.7), channel_id=1, source_target_pairs={{1,0},{2,1},{3,2},{4,3},{5,4},{6,5},{7,6},{8,7},{9,8},{10,9},{11,1... | collective-permute-start | bytes 1769480 | tf_op jit(solution)/shard_map/ppermute | solution.py:103
  153.1 30.5 %collective-permute-start.6 = (f32[384,384]{1,0:T(8,128)S(1)}, f32[384,384]{1,0:T(8,128)S(1)}, u32[]{:S(2)}, u32[]{:S(2)}) collective-permute-start(f32[384,384]{1,0:T(8,128)S(1)} %fusion.47), channel_id=1, source_target_pairs={{2,1},{4,3},{6,5},{8,7},{10,9},{12,11},{14,13},{16,15},{18,17},{20... | collective-permute-start | bytes 1769480 | tf_op jit(solution)/shard_map/ppermute | solution.py:103
  165.8 24.9 %collective-permute-start.5 = (f32[384,384]{1,0:T(8,128)S(1)}, f32[384,384]{1,0:T(8,128)S(1)}, u32[]{:S(2)}, u32[]{:S(2)}) collective-permute-start(f32[384,384]{1,0:T(8,128)S(1)} %fusion.45), channel_id=1, source_target_pairs={{0,1},{2,3},{4,5},{6,7},{8,9},{10,11},{12,13},{14,15},{16,17},{18,... | collective-permute-start | bytes 1769480 | tf_op jit(solution)/shard_map/ppermute | solution.py:103
  168.5 52.0 %collective-permute-start.32 = (f32[384,128]{1,0:T(8,128)}, f32[384,128]{1,0:T(8,128)}, u32[]{:S(2)}, u32[]{:S(2)}) collective-permute-start(f32[384,128]{1,0:T(8,128)} %fusion.82), channel_id=1, source_target_pairs={{0,1},{2,3},{4,5},{6,7},{8,9},{10,11},{12,13},{14,15},{16,17},{18,... | collective-permute-start | bytes 589832 | tf_op jit(solution)/shard_map/ppermute | solution.py:103
  173.2 47.3 %collective-permute-start.33 = (f32[384,128]{1,0:T(8,128)}, f32[384,128]{1,0:T(8,128)}, u32[]{:S(2)}, u32[]{:S(2)}) collective-permute-start(f32[384,128]{1,0:T(8,128)} %fusion.83), channel_id=1, source_target_pairs={{2,1},{4,3},{6,5},{8,7},{10,9},{12,11},{14,13},{16,15},{18,17},{20... | collective-permute-start | bytes 589832 | tf_op jit(solution)/shard_map/ppermute | solution.py:103
  180.1 45.9 %collective-permute-start.4 = (f32[384,384]{1,0:T(8,128)}, f32[384,384]{1,0:T(8,128)}, u32[]{:S(2)}, u32[]{:S(2)}) collective-permute-start(f32[384,384]{1,0:T(8,128)} %fusion.43), channel_id=1, source_target_pairs={{2,1},{4,3},{6,5},{8,7},{10,9},{12,11},{14,13},{16,15},{18,17},{20... | collective-permute-start | bytes 1769480 | tf_op jit(solution)/shard_map/ppermute | solution.py:103
  183.6 42.3 %collective-permute-start.3 = (f32[384,384]{1,0:T(8,128)}, f32[384,384]{1,0:T(8,128)}, u32[]{:S(2)}, u32[]{:S(2)}) collective-permute-start(f32[384,384]{1,0:T(8,128)} %fusion.42), channel_id=1, source_target_pairs={{0,1},{2,3},{4,5},{6,7},{8,9},{10,11},{12,13},{14,15},{16,17},{18,... | collective-permute-start | bytes 1769480 | tf_op jit(solution)/shard_map/ppermute | solution.py:103
  190.7 44.4 %collective-permute-start.8 = (f32[384,384]{1,0:T(8,128)S(1)}, f32[384,384]{1,0:T(8,128)S(1)}, u32[]{:S(2)}, u32[]{:S(2)}) collective-permute-start(f32[384,384]{1,0:T(8,128)S(1)} %negate_select_fusion.3), channel_id=1, source_target_pairs={{3,1},{7,5},{11,9},{15,13},{19,17},{23,21},{27,25},{31,29}} | collective-permute-start | bytes 1769480 | tf_op jit(solution)/shard_map/ppermute | solution.py:103
  244.1 41.3 %collective-permute-start.10 = (f32[384,384]{1,0:T(8,128)}, f32[384,384]{1,0:T(8,128)}, u32[]{:S(2)}, u32[]{:S(2)}) collective-permute-start(f32[384,384]{1,0:T(8,128)} %fusion.51), channel_id=1, source_target_pairs={{5,3},{9,7},{13,11},{17,15},{21,19},{25,23},{29,27}} | collective-permute-start | bytes 1769480 | tf_op jit(solution)/shard_map/ppermute | solution.py:103
  245.5 39.8 %collective-permute-start.9 = (f32[384,384]{1,0:T(8,128)}, f32[384,384]{1,0:T(8,128)}, u32[]{:S(2)}, u32[]{:S(2)}) collective-permute-start(f32[384,384]{1,0:T(8,128)} %fusion.50), channel_id=1, source_target_pairs={{1,3},{5,7},{9,11},{13,15},{17,19},{21,23},{25,27},{29,31}} | collective-permute-start | bytes 1769480 | tf_op jit(solution)/shard_map/ppermute | solution.py:103
  248.8 49.0 %collective-permute-start.14 = (f32[384,384]{1,0:T(8,128)S(1)}, f32[384,384]{1,0:T(8,128)S(1)}, u32[]{:S(2)}, u32[]{:S(2)}) collective-permute-start(f32[384,384]{1,0:T(8,128)S(1)} %negate_select_fusion.2), channel_id=1, source_target_pairs={{7,3},{15,11},{23,19},{31,27}} | collective-permute-start | bytes 1769480 | tf_op jit(solution)/shard_map/ppermute | solution.py:103
  282.5 58.1 %collective-permute-start.37 = (f32[384,128]{1,0:T(8,128)}, f32[384,128]{1,0:T(8,128)}, u32[]{:S(2)}, u32[]{:S(2)}) collective-permute-start(f32[384,128]{1,0:T(8,128)} %fusion.88), channel_id=1, source_target_pairs={{11,7},{19,15},{27,23}} | collective-permute-start | bytes 589832 | tf_op jit(solution)/shard_map/ppermute | solution.py:103
  291.7 53.3 %collective-permute-start.16 = (f32[384,384]{1,0:T(8,128)}, f32[384,384]{1,0:T(8,128)}, u32[]{:S(2)}, u32[]{:S(2)}) collective-permute-start(f32[384,384]{1,0:T(8,128)} %fusion.59), channel_id=1, source_target_pairs={{11,7},{19,15},{27,23}} | collective-permute-start | bytes 1769480 | tf_op jit(solution)/shard_map/ppermute | solution.py:103
  307.0 33.6 %collective-permute-start.36 = (f32[384,128]{1,0:T(8,128)}, f32[384,128]{1,0:T(8,128)}, u32[]{:S(2)}, u32[]{:S(2)}) collective-permute-start(f32[384,128]{1,0:T(8,128)} %fusion.87), channel_id=1, source_target_pairs={{3,7},{11,15},{19,23},{27,31}} | collective-permute-start | bytes 589832 | tf_op jit(solution)/shard_map/ppermute | solution.py:103
  308.5 36.5 %collective-permute-start.15 = (f32[384,384]{1,0:T(8,128)}, f32[384,384]{1,0:T(8,128)}, u32[]{:S(2)}, u32[]{:S(2)}) collective-permute-start(f32[384,384]{1,0:T(8,128)} %fusion.58), channel_id=1, source_target_pairs={{3,7},{11,15},{19,23},{27,31}} | collective-permute-start | bytes 1769480 | tf_op jit(solution)/shard_map/ppermute | solution.py:103
  310.0 48.3 %collective-permute-start.20 = (f32[384,384]{1,0:T(8,128)S(1)}, f32[384,384]{1,0:T(8,128)}, u32[]{:S(2)}, u32[]{:S(2)}) collective-permute-start(f32[384,384]{1,0:T(8,128)S(1)} %negate_select_fusion.1), channel_id=1, source_target_pairs={{15,7},{31,23}} | collective-permute-start | bytes 1769480 | tf_op jit(solution)/shard_map/ppermute | solution.py:103
  349.6 23.0 %collective-permute-start.39 = (f32[384,128]{1,0:T(8,128)S(1)}, f32[384,128]{1,0:T(8,128)S(1)}, u32[]{:S(2)}, u32[]{:S(2)}) collective-permute-start(f32[384,128]{1,0:T(8,128)S(1)} %fusion.90), channel_id=1, source_target_pairs={{23,15}} | collective-permute-start | bytes 589832 | tf_op jit(solution)/shard_map/ppermute | solution.py:103
  353.9 25.4 %collective-permute-start.24 = (f32[384,384]{1,0:T(8,128)S(1)}, f32[384,384]{1,0:T(8,128)S(1)}, u32[]{:S(2)}, u32[]{:S(2)}) collective-permute-start(f32[384,384]{1,0:T(8,128)S(1)} %fusion.71), channel_id=1, source_target_pairs={{23,15}} | collective-permute-start | bytes 1769480 | tf_op jit(solution)/shard_map/ppermute | solution.py:103
  372.6 39.9 %collective-permute-start.22 = (f32[384,384]{1,0:T(8,128)}, f32[384,384]{1,0:T(8,128)}, u32[]{:S(2)}, u32[]{:S(2)}) collective-permute-start(f32[384,384]{1,0:T(8,128)} %fusion.67), channel_id=1, source_target_pairs={{23,15}} | collective-permute-start | bytes 1769480 | tf_op jit(solution)/shard_map/ppermute | solution.py:103
  374.1 38.5 %collective-permute-start.21 = (f32[384,384]{1,0:T(8,128)}, f32[384,384]{1,0:T(8,128)}, u32[]{:S(2)}, u32[]{:S(2)}) collective-permute-start(f32[384,384]{1,0:T(8,128)} %fusion.66), channel_id=1, source_target_pairs={{7,15},{23,31}} | collective-permute-start | bytes 1769480 | tf_op jit(solution)/shard_map/ppermute | solution.py:103
  377.4 46.6 %collective-permute-start.26 = (f32[384,384]{1,0:T(8,128)S(1)}, f32[384,384]{1,0:T(8,128)}, u32[]{:S(2)}, u32[]{:S(2)}) collective-permute-start(f32[384,384]{1,0:T(8,128)S(1)} %negate_select_fusion), channel_id=1, source_target_pairs={{31,15}} | collective-permute-start | bytes 1769480 | tf_op jit(solution)/shard_map/ppermute | solution.py:103
  418.6 22.6 %collective-permute-start.30 = (f32[384,384]{1,0:T(8,128)S(1)}, f32[384,384]{1,0:T(8,128)S(1)}, u32[]{:S(2)}, u32[]{:S(2)}) collective-permute-start(f32[384,384]{1,0:T(8,128)S(1)} %fusion.79), channel_id=1, source_target_pairs={} | collective-permute-start | bytes 1769480 | tf_op jit(solution)/shard_map/ppermute | solution.py:103
  431.4 43.3 %collective-permute-start.41 = (f32[384,128]{1,0:T(8,128)}, f32[384,128]{1,0:T(8,128)}, u32[]{:S(2)}, u32[]{:S(2)}) collective-permute-start(f32[384,128]{1,0:T(8,128)} %fusion.93), channel_id=1, source_target_pairs={} | collective-permute-start | bytes 589832 | tf_op jit(solution)/shard_map/ppermute | solution.py:103
  432.9 39.1 %collective-permute-start.28 = (f32[384,384]{1,0:T(8,128)}, f32[384,384]{1,0:T(8,128)}, u32[]{:S(2)}, u32[]{:S(2)}) collective-permute-start(f32[384,384]{1,0:T(8,128)} %fusion.75), channel_id=1, source_target_pairs={} | collective-permute-start | bytes 1769480 | tf_op jit(solution)/shard_map/ppermute | solution.py:103
  436.8 38.0 %collective-permute-start.40 = (f32[384,128]{1,0:T(8,128)}, f32[384,128]{1,0:T(8,128)}, u32[]{:S(2)}, u32[]{:S(2)}) collective-permute-start(f32[384,128]{1,0:T(8,128)} %fusion.92), channel_id=1, source_target_pairs={{15,31}} | collective-permute-start | bytes 589832 | tf_op jit(solution)/shard_map/ppermute | solution.py:103
  441.3 30.8 %collective-permute-start.27 = (f32[384,384]{1,0:T(8,128)}, f32[384,384]{1,0:T(8,128)}, u32[]{:S(2)}, u32[]{:S(2)}) collective-permute-start(f32[384,384]{1,0:T(8,128)} %fusion.74), channel_id=1, source_target_pairs={{15,31}} | collective-permute-start | bytes 1769480 | tf_op jit(solution)/shard_map/ppermute | solution.py:103
  706.0 25.5 %collective-permute-start.50 = (f32[384,128]{1,0:T(8,128)S(1)}, f32[384,128]{1,0:T(8,128)S(1)}, u32[]{:S(2)}, u32[]{:S(2)}) collective-permute-start(f32[384,128]{1,0:T(8,128)S(1)} %subtract_select_fusion.1), channel_id=1, source_target_pairs={{1,2},{3,4},{5,6},{7,8},{9,10},{11,12},{13,14},{15,16},{17,18},{19... | collective-permute-start | bytes 589832 | tf_op jit(solution)/shard_map/ppermute | solution.py:103
  708.1 26.4 %collective-permute-start.51 = (f32[384,128]{1,0:T(8,128)S(1)}, f32[384,128]{1,0:T(8,128)S(1)}, u32[]{:S(2)}, u32[]{:S(2)}) collective-permute-start(f32[384,128]{1,0:T(8,128)S(1)} %subtract_select_fusion.1), channel_id=1, source_target_pairs={{1,0},{3,2},{5,4},{7,6},{9,8},{11,10},{13,12},{15,14},{17,16},{19,... | collective-permute-start | bytes 589832 | tf_op jit(solution)/shard_map/ppermute | solution.py:103
  (116 other events, 1327.6 us)
Sparse Core Ops, SparseCore 0:
  482.6 175.0 all-reduce.2

commit v2 on v1

--- a/solution.py
+++ b/solution.py
@@ -7,41 +7,75 @@
 
 AXES = ("long", "short")
 PREC = lax.Precision.HIGHEST
+FAST = lax.Precision.HIGHEST
 LANES = 128
 SUBLANES = 8
 
 
-def gram_prod(left, right):
-    return jnp.einsum("ji,jk->ik", left, right, precision=PREC)
-
-
-def mat_prod(left, right):
-    return jnp.matmul(left, right, precision=PREC)
-
-
-def pivot_pair(tiles, first, lane, sub):
+def gram_prod(left, right, precision=FAST):
+    return jnp.einsum("ji,jk->ik", left, right, precision=precision)
+
+
+def mat_prod(left, right, precision=FAST):
+    return jnp.matmul(left, right, precision=precision)
+
+
+def inverse_two(a, b, c):
+    inv = 1.0 / (a * c - b * b)
+    return c * inv, -(b * inv), a * inv
+
+
+def pivot_four(tiles, first, lane, sub):
     group, row = divmod(first, SUBLANES)
     shape = (SUBLANES, LANES)
-    col0 = [jnp.broadcast_to(t[:, first : first + 1], shape) for t in tiles]
-    col1 = [jnp.broadcast_to(t[:, first + 1 : first + 2], shape) for t in tiles]
-    at0, at1 = lane == first, lane == first + 1
-    a = col0[group][row : row + 1, :]
-    b = col1[group][row : row + 1, :]
-    c = col1[group][row + 1 : row + 2, :]
-    inv = 1.0 / (a * c - b * b)
-    row0 = tiles[group][row : row + 1, :]
-    row1 = tiles[group][row + 1 : row + 2, :]
-    at0_row, at1_row = at0[:1], at1[:1]
-    row0 = jnp.where(at0_row, 1.0, jnp.where(at1_row, 0.0, row0))
-    row1 = jnp.where(at1_row, 1.0, jnp.where(at0_row, 0.0, row1))
-    q0 = jnp.broadcast_to((c * row0 - b * row1) * inv, shape)
-    q1 = jnp.broadcast_to((a * row1 - b * row0) * inv, shape)
-    both = jnp.logical_or(at0, at1)
+    cols = [
+        [jnp.broadcast_to(t[:, first + k : first + k + 1], shape) for t in tiles] for k in range(4)
+    ]
+
+    def entry(i, k):
+        return cols[k][group][row + i : row + i + 1, :]
+
+    a00, a01, a11 = inverse_two(entry(0, 0), entry(0, 1), entry(1, 1))
+    b00, b01, b10, b11 = entry(0, 2), entry(0, 3), entry(1, 2), entry(1, 3)
+    m00, m01 = a00 * b00 + a01 * b10, a00 * b01 + a01 * b11
+    m10, m11 = a01 * b00 + a11 * b10, a01 * b01 + a11 * b11
+    s00, s01, s11 = inverse_two(
+        entry(2, 2) - (b00 * m00 + b10 * m10),
+        entry(2, 3) - (b00 * m01 + b10 * m11),
+        entry(3, 3) - (b01 * m01 + b11 * m11),
+    )
+    u00, u01 = m00 * s00 + m01 * s01, m00 * s01 + m01 * s11
+    u10, u11 = m10 * s00 + m11 * s01, m10 * s01 + m11 * s11
+    t01 = a01 + (u00 * m10 + u01 * m11)
+    pivot_inverse = (
+        (a00 + (u00 * m00 + u01 * m01), t01, -u00, -u01),
+        (t01, a11 + (u10 * m10 + u11 * m11), -u10, -u11),
+        (-u00, -u10, s00, s01),
+        (-u01, -u11, s01, s11),
+    )
+    inside = jnp.logical_and(lane >= first, lane < first + 4)
+    rows = [
+        jnp.where(
+            inside[:1],
+            jnp.where(lane[:1] == first + k, 1.0, 0.0),
+            tiles[group][row + k : row + k + 1, :],
+        )
+        for k in range(4)
+    ]
+    scaled = [
+        jnp.broadcast_to(
+            (p[0] * rows[0] + p[1] * rows[1]) + (p[2] * rows[2] + p[3] * rows[3]), shape
+        )
+        for p in pivot_inverse
+    ]
     out = []
     for place, tile in enumerate(tiles):
-        new = jnp.where(both, 0.0, tile) - col0[place] * q0 - col1[place] * q1
+        new = jnp.where(inside, 0.0, tile)
+        for k in range(4):
+            new = new - cols[k][place] * scaled[k]
         if place == group:
-            new = jnp.where(sub == row, q0, jnp.where(sub == row + 1, q1, new))
+            for k in range(4):
+                new = jnp.where(sub == row + k, scaled[k], new)
         out.append(new)
     return out
 
@@ -59,8 +93,8 @@
             o_ref[pl.ds(pl.multiple_of(at + SUBLANES * g, SUBLANES), SUBLANES), here]
             for g in range(LANES // SUBLANES)
         ]
-        for first in range(0, LANES, 2):
-            tiles = pivot_pair(tiles, first, lane, sub)
+        for first in range(0, LANES, 4):
+            tiles = pivot_four(tiles, first, lane, sub)
         pivot = jnp.concatenate(tiles, axis=0)
         rows = o_ref[here, :]
         columns = o_ref[:, here]
@@ -104,10 +138,10 @@
 
     weighted_trans = innovation[:, :, None] * transition
     weighted_effect = innovation[:, :, None] * effects
-    succ_diag = [gram_prod(transition[t], weighted_trans[t]) for t in range(block_count)]
-    succ_arrow = [gram_prod(transition[t], weighted_effect[t]) for t in range(block_count)]
+    succ_diag = [gram_prod(transition[t], weighted_trans[t], PREC) for t in range(block_count)]
+    succ_arrow = [gram_prod(transition[t], weighted_effect[t], PREC) for t in range(block_count)]
     tip_terms = gram_prod(
-        effects.reshape(-1, tip_width), weighted_effect.reshape(-1, tip_width)
+        effects.reshape(-1, tip_width), weighted_effect.reshape(-1, tip_width), PREC
     )
     global_block = position * block_count + jnp.arange(block_count)
     couple = -weighted_trans * jnp.where(global_block == 0, 0.0, 1.0)[:, None, None]
@@ -133,7 +167,7 @@
             diag_item = diag_item + succ_diag[t + 1]
             arrow_item = arrow_item + succ_arrow[t + 1]
             inverse = spd_inverse(diag_item)
-            link = jnp.einsum("ij,kj->ik", inverse, couple[t + 1], precision=PREC)
+            link = jnp.einsum("ij,kj->ik", inverse, couple[t + 1], precision=FAST)
             y_left = mat_prod(inverse, left_item)
             y_arrow = mat_prod(inverse, arrow_item)
             y_rhs = mat_prod(inverse, rhs_item)
@@ -180,8 +214,10 @@
         arrow_left = send(gram_prod(node_couple, y_arrow), leftward)
         rhs_right = send(gram_prod(right_item, y_rhs), rightward)
         rhs_left = send(gram_prod(node_couple, y_rhs), leftward)
-        tip_terms = tip_terms - jnp.where(drop, gram_prod(node_arrow, y_arrow), 0.0)
-        tip_rhs_terms = tip_rhs_terms - jnp.where(drop, gram_prod(node_arrow, y_rhs), 0.0)
+        tip_passed = send(tip_terms - gram_prod(node_arrow, y_arrow), rightward)
+        tip_rhs_passed = send(tip_rhs_terms - gram_prod(node_arrow, y_rhs), rightward)
+        tip_terms = tip_terms + tip_passed
+        tip_rhs_terms = tip_rhs_terms + tip_rhs_passed
         levels.append((drop, back_left, back_right, y_left, y_right, y_arrow, y_rhs))
         node_diag = node_diag - diag_right - diag_left
         node_couple = jnp.where(fed, -new_couple, node_couple)
@@ -193,17 +229,22 @@
     inverse = spd_inverse(node_diag)
     y_arrow = mat_prod(inverse, node_arrow)
     y_rhs = mat_prod(inverse, node_rhs)
-    tip_terms = tip_terms - jnp.where(final, gram_prod(node_arrow, y_arrow), 0.0)
-    tip_rhs_terms = tip_rhs_terms - jnp.where(final, gram_prod(node_arrow, y_rhs), 0.0)
-    tip_total, tip_rhs_total = lax.psum((tip_terms, tip_rhs_terms), AXES)
-    tip_solution = mat_prod(spd_inverse(tip_total + jnp.diag(prior)), tip_rhs_total + tip_right)
-
-    node_x = y_rhs - mat_prod(y_arrow, tip_solution)
+    tip_total = tip_terms - gram_prod(node_arrow, y_arrow) + jnp.diag(prior)
+    tip_rhs_total = tip_rhs_terms - gram_prod(node_arrow, y_rhs) + tip_right
+    tip_found = mat_prod(spd_inverse(tip_total), tip_rhs_total)
+    tip_solution = jnp.where(final, tip_found, 0.0)
+    node_x = jnp.where(final, y_rhs - mat_prod(y_arrow, tip_solution), 0.0)
+
     for drop, back_left, back_right, y_left, y_right, y_arrow, y_rhs in reversed(levels):
-        base = y_rhs - mat_prod(y_arrow, tip_solution)
+        tip_solution = tip_solution + send(tip_solution, back_right)
         left_x = send(node_x, back_left)
         right_x = send(node_x, back_right)
-        value = base - mat_prod(y_left, left_x) - mat_prod(y_right, right_x)
+        value = (
+            y_rhs
+            - mat_prod(y_arrow, tip_solution)
+            - mat_prod(y_left, left_x)
+            - mat_prod(y_right, right_x)
+        )
         node_x = jnp.where(drop, value, node_x)
     left_x = send(node_x, [(i, i + 1) for i in range(total - 1)])
     outs = [node_x]

time: 763 us -> 671 us (0.88)
  waiting for transfers between devices: 229 us -> 32.6 us
  starting transfers between devices: 94.7 us -> 234 us
  Pallas kernels: 226 us -> 192 us
  between operations: 16.6 us -> 3.09 us
    psum x1 -> x0, waiting for transfers between devices: 175 us -> none  [body(): tip_total, tip_rhs_total = lax.psum((tip_terms, tip_rhs_terms), AXES)]
    ppermute x53 -> x68, starting transfers between devices: 94.6 us -> 234 us  [send(): return lax.ppermute(values, AXES, pairs)]
    pallas_call x8, Pallas kernels: 226 us -> 192 us  [spd_inverse(): pl.pallas_call(inverse_kernel, out_shape=jax.ShapeDtypeStruct(matrix.shap...]
    ppermute x53 -> x68, waiting for transfers between devices: 53.6 us -> 32.6 us  [send(): return lax.ppermute(values, AXES, pairs)]
    add x1 -> x13, other arithmetic: 2 us -> 10.1 us  [the longest x5 4.54 us: body(): tip_solution = tip_solution + send(tip_solution, back_right)]
  transfers between devices with their start and end apart: 54 -> 68, of which waited for: 6 -> 5; matrix products, arithmetic and copies ran while one was open for 21% -> 27% of each run, Pallas kernels for 22% -> 25%
where the time goes in v2:
time: 671 us; the launch traced here: 662 us
  starting transfers between devices  234 us (35%)
  Pallas kernels  192 us (29%)
  matrix products  165 us (25%)
  waiting for transfers between devices  32.6 us (5%)
  other arithmetic  29.8 us (4%)
    ppermute x68, starting transfers between devices, send(): return lax.ppermute(values, AXES, pairs)  234 us
    pallas_call x8, Pallas kernels, spd_inverse(): pl.pallas_call(inverse_kernel, out_shape=jax.ShapeDtypeStruct(matrix.shap...  192 us
    dot_general x56, matrix products, gram_prod(): return jnp.einsum('ji,jk->ik', left, right, precision=precision)  94.9 us
    dot_general x49, matrix products, mat_prod(): return jnp.matmul(left, right, precision=precision)  68.2 us
    ppermute x68, waiting for transfers between devices, send(): return lax.ppermute(values, AXES, pairs)  32.6 us
  transfers between devices with their start and end apart: 68, of which 5 were waited for; matrix products, arithmetic and copies ran while one was open for 27% of the time, Pallas kernels for 25%

profile of v2, /device:TPU:1, one launch (start us, length us, event | category | flops | bytes accessed | tf_op | source)
XLA Modules:
  0.0 662.0 jit_solution(5763246498834404297)
XLA Ops:
  1.4 3.1 negate_multiply_fusion
  8.1 24.0 %spd_inverse.8 = f32[384,384]{1,0:T(8,128)} custom-call(f32[384,384]{1,0:T(8,128)} %fusion.5.a_ref), custom_call_target="tpu_custom_call" | custom-call | flops 16986931200 | bytes 1179648 | tf_op jit(solution)/shard_map/spd_inverse/pallas_call | solution.py:117
  35.8 8.7 %collective-permute-start.36 = (f32[384,128]{1,0:T(8,128)}, f32[384,128]{1,0:T(8,128)}, u32[]{:S(2)}, u32[]{:S(2)}) collective-permute-start(f32[384,128]{1,0:T(8,128)} %convolution_subtract_fusion.23), channel_id=1, source_target_pairs={{1,0},{2,1},{3,2},{4,3},{5,4},{6,5},{7,6},{8,7},{9,8},{10,9},{11,1... | collective-permute-start | bytes 589832 | tf_op jit(solution)/shard_map/ppermute | solution.py:137
  50.7 7.4 %collective-permute-start = (f32[384,384]{1,0:T(8,128)}, f32[384,384]{1,0:T(8,128)}, u32[]{:S(2)}, u32[]{:S(2)}) collective-permute-start(f32[384,384]{1,0:T(8,128)} %fusion.1), channel_id=1, source_target_pairs={{1,0},{2,1},{3,2},{4,3},{5,4},{6,5},{7,6},{8,7},{9,8},{10,9},{11,1... | collective-permute-start | bytes 1769480 | tf_op jit(solution)/shard_map/ppermute | solution.py:137
  65.6 8.3 %collective-permute-start.1 = (f32[384,384]{1,0:T(8,128)}, f32[384,384]{1,0:T(8,128)}, u32[]{:S(2)}, u32[]{:S(2)}) collective-permute-start(f32[384,384]{1,0:T(8,128)} %fusion.3), channel_id=1, source_target_pairs={{1,0},{2,1},{3,2},{4,3},{5,4},{6,5},{7,6},{8,7},{9,8},{10,9},{11,1... | collective-permute-start | bytes 1769480 | tf_op jit(solution)/shard_map/ppermute | solution.py:137
  80.5 2.9 convolution_negate_fusion.1
  85.1 13.2 %collective-permute-done.1 = f32[384,384]{1,0:T(8,128)} collective-permute-done((f32[384,384]{1,0:T(8,128)}, f32[384,384]{1,0:T(8,128)}, u32[]{:S(2)}, u32[]{:S(2)}) %collective-permute-start.1) | collective-permute-done | bytes 589856 | tf_op jit(solution)/shard_map/ppermute | solution.py:137
  98.3 3.1 fusion.2.a_ref
  101.4 24.2 %spd_inverse.9 = f32[384,384]{1,0:T(8,128)} custom-call(f32[384,384]{1,0:T(8,128)} %fusion.2.a_ref), custom_call_target="tpu_custom_call" | custom-call | flops 16986931200 | bytes 1179648 | tf_op jit(solution)/shard_map/spd_inverse/pallas_call | solution.py:117
  127.4 2.6 fusion
  138.4 7.4 %collective-permute-start.38 = (f32[384,128]{1,0:T(8,128)}, f32[384,128]{1,0:T(8,128)}, u32[]{:S(2)}, u32[]{:S(2)}) collective-permute-start(f32[384,128]{1,0:T(8,128)} %fusion.89), channel_id=1, source_target_pairs={{0,1},{2,3},{4,5},{6,7},{8,9},{10,11},{12,13},{14,15},{16,17},{18,... | collective-permute-start | bytes 589832 | tf_op jit(solution)/shard_map/ppermute | solution.py:137
  145.7 6.7 %collective-permute-start.39 = (f32[384,128]{1,0:T(8,128)}, f32[384,128]{1,0:T(8,128)}, u32[]{:S(2)}, u32[]{:S(2)}) collective-permute-start(f32[384,128]{1,0:T(8,128)} %fusion.90), channel_id=1, source_target_pairs={{2,1},{4,3},{6,5},{8,7},{10,9},{12,11},{14,13},{16,15},{18,17},{20... | collective-permute-start | bytes 589832 | tf_op jit(solution)/shard_map/ppermute | solution.py:137
  155.9 6.1 collective-permute-start.7
  165.4 3.2 collective-permute-start.6
  175.1 6.2 collective-permute-start.5
  182.1 3.4 collective-permute-start.4
  187.7 24.0 %spd_inverse.10 = f32[384,384]{1,0:T(8,128)} custom-call(f32[384,384]{1,0:T(8,128)} %subtract_subtract_fusion.8.a_ref), custom_call_target="tpu_custom_call" | custom-call | flops 16986931200 | bytes 1179648 | tf_op jit(solution)/shard_map/spd_inverse/pallas_call | solution.py:117
  213.7 3.7 collective-permute-start.2
  237.5 31.3 %collective-permute-start.41 = (f32[384,128]{1,0:T(8,128)S(1)}, f32[384,128]{1,0:T(8,128)S(1)}, u32[]{:S(2)}, u32[]{:S(2)}) collective-permute-start(f32[384,128]{1,0:T(8,128)S(1)} %fusion.91), channel_id=1, source_target_pairs={{1,3},{5,7},{9,11},{13,15},{17,19},{21,23},{25,27},{29,31}} | collective-permute-start | bytes 589832 | tf_op jit(solution)/shard_map/ppermute | solution.py:137
  284.3 24.0 %spd_inverse.11 = f32[384,384]{1,0:T(8,128)} custom-call(f32[384,384]{1,0:T(8,128)} %subtract_subtract_fusion.6.a_ref), custom_call_target="tpu_custom_call" | custom-call | flops 16986931200 | bytes 1179648 | tf_op jit(solution)/shard_map/spd_inverse/pallas_call | solution.py:117
  342.2 24.0 %spd_inverse.12 = f32[384,384]{1,0:T(8,128)} custom-call(f32[384,384]{1,0:T(8,128)} %subtract_subtract_fusion.4.a_ref), custom_call_target="tpu_custom_call" | custom-call | flops 16986931200 | bytes 1179648 | tf_op jit(solution)/shard_map/spd_inverse/pallas_call | solution.py:117
  401.3 24.1 %spd_inverse.13 = f32[384,384]{1,0:T(8,128)} custom-call(f32[384,384]{1,0:T(8,128)} %subtract_subtract_fusion.2.a_ref), custom_call_target="tpu_custom_call" | custom-call | flops 16986931200 | bytes 1179648 | tf_op jit(solution)/shard_map/spd_inverse/pallas_call | solution.py:117
  454.6 3.1 fusion.81
  461.6 24.0 %spd_inverse.14 = f32[384,384]{1,0:T(8,128)} custom-call(f32[384,384]{1,0:T(8,128)} %subtract_subtract_fusion.a_ref), custom_call_target="tpu_custom_call" | custom-call | flops 16986931200 | bytes 1179648 | tf_op jit(solution)/shard_map/spd_inverse/pallas_call | solution.py:117
  490.3 3.2 select_add_fusion.a_ref
  493.5 24.0 %spd_inverse.15 = f32[384,384]{1,0:T(8,128)} custom-call(f32[384,384]{1,0:T(8,128)} %select_add_fusion.a_ref), custom_call_target="tpu_custom_call" | custom-call | flops 16986931200 | bytes 1179648 | tf_op jit(solution)/shard_map/spd_inverse/pallas_call | solution.py:117
  553.5 59.5 %collective-permute-start.64 = (f32[384,128]{1,0:T(8,128)S(1)}, f32[384,128]{1,0:T(8,128)S(1)}, u32[]{:S(2)}, u32[]{:S(2)}) collective-permute-start(f32[384,128]{1,0:T(8,128)S(1)} %fusion.20), channel_id=1, source_target_pairs={{3,1},{7,5},{11,9},{15,13},{19,17},{23,21},{27,25},{31,29}} | collective-permute-start | bytes 589832 | tf_op jit(solution)/shard_map/ppermute | solution.py:137
  617.2 13.6 %collective-permute-start.66 = (f32[384,128]{1,0:T(8,128)S(1)}, f32[384,128]{1,0:T(8,128)S(1)}, u32[]{:S(2)}, u32[]{:S(2)}) collective-permute-start(f32[384,128]{1,0:T(8,128)S(1)} %fusion.22), channel_id=1, source_target_pairs={{1,0},{3,2},{5,4},{7,6},{9,8},{11,10},{13,12},{15,14},{17,16},{19,... | collective-permute-start | bytes 589832 | tf_op jit(solution)/shard_map/ppermute | solution.py:137
  630.8 7.0 %collective-permute-start.65 = (f32[384,128]{1,0:T(8,128)S(1)}, f32[384,128]{1,0:T(8,128)S(1)}, u32[]{:S(2)}, u32[]{:S(2)}) collective-permute-start(f32[384,128]{1,0:T(8,128)S(1)} %fusion.22), channel_id=1, source_target_pairs={{1,2},{3,4},{5,6},{7,8},{9,10},{11,12},{13,14},{15,16},{17,18},{19... | collective-permute-start | bytes 589832 | tf_op jit(solution)/shard_map/ppermute | solution.py:137
  639.3 7.6 %collective-permute-done.65 = f32[384,128]{1,0:T(8,128)S(1)} collective-permute-done((f32[384,128]{1,0:T(8,128)S(1)}, f32[384,128]{1,0:T(8,128)S(1)}, u32[]{:S(2)}, u32[]{:S(2)}) %collective-permute-start.65) | collective-permute-done | bytes 196640 | tf_op jit(solution)/shard_map/ppermute | solution.py:137
  648.2 3.8 collective-permute-start.67
  652.6 7.7 %collective-permute-done.67 = f32[384,128]{1,0:T(8,128)S(1)} collective-permute-done((f32[384,128]{1,0:T(8,128)S(1)}, f32[384,128]{1,0:T(8,128)S(1)}, u32[]{:S(2)}, u32[]{:S(2)}) %collective-permute-start.67) | collective-permute-done | bytes 196640 | tf_op jit(solution)/shard_map/ppermute | solution.py:137
  (424 shorter events, 243.7 us)
Async XLA Ops:
  35.8 47.6 %collective-permute-start.36 = (f32[384,128]{1,0:T(8,128)}, f32[384,128]{1,0:T(8,128)}, u32[]{:S(2)}, u32[]{:S(2)}) collective-permute-start(f32[384,128]{1,0:T(8,128)} %convolution_subtract_fusion.23), channel_id=1, source_target_pairs={{1,0},{2,1},{3,2},{4,3},{5,4},{6,5},{7,6},{8,7},{9,8},{10,9},{11,1... | collective-permute-start | bytes 589832 | tf_op jit(solution)/shard_map/ppermute | solution.py:137
  50.7 76.7 %collective-permute-start = (f32[384,384]{1,0:T(8,128)}, f32[384,384]{1,0:T(8,128)}, u32[]{:S(2)}, u32[]{:S(2)}) collective-permute-start(f32[384,384]{1,0:T(8,128)} %fusion.1), channel_id=1, source_target_pairs={{1,0},{2,1},{3,2},{4,3},{5,4},{6,5},{7,6},{8,7},{9,8},{10,9},{11,1... | collective-permute-start | bytes 1769480 | tf_op jit(solution)/shard_map/ppermute | solution.py:137
  60.6 76.4 %collective-permute-start.3 = (f32[384,384]{1,0:T(8,128)S(1)}, f32[384,384]{1,0:T(8,128)S(1)}, u32[]{:S(2)}, u32[]{:S(2)}) collective-permute-start(f32[384,384]{1,0:T(8,128)S(1)} %convolution_negate_fusion), channel_id=1, source_target_pairs={{1,0},{3,2},{5,4},{7,6},{9,8},{11,10},{13,12},{15,14},{17,16},{19,... | collective-permute-start | bytes 1769480 | tf_op jit(solution)/shard_map/ppermute | solution.py:137
  65.6 32.7 %collective-permute-start.1 = (f32[384,384]{1,0:T(8,128)}, f32[384,384]{1,0:T(8,128)}, u32[]{:S(2)}, u32[]{:S(2)}) collective-permute-start(f32[384,384]{1,0:T(8,128)} %fusion.3), channel_id=1, source_target_pairs={{1,0},{2,1},{3,2},{4,3},{5,4},{6,5},{7,6},{8,7},{9,8},{10,9},{11,1... | collective-permute-start | bytes 1769480 | tf_op jit(solution)/shard_map/ppermute | solution.py:137
  132.9 42.2 %collective-permute-start.37 = (f32[384,128]{1,0:T(8,128)S(1)}, f32[384,128]{1,0:T(8,128)S(1)}, u32[]{:S(2)}, u32[]{:S(2)}) collective-permute-start(f32[384,128]{1,0:T(8,128)S(1)} %convolution_subtract_fusion.22), channel_id=1, source_target_pairs={{0,1},{2,3},{4,5},{6,7},{8,9},{10,11},{12,13},{14,15},{16,17},{18,... | collective-permute-start | bytes 589832 | tf_op jit(solution)/shard_map/ppermute | solution.py:137
  138.4 81.6 %collective-permute-start.38 = (f32[384,128]{1,0:T(8,128)}, f32[384,128]{1,0:T(8,128)}, u32[]{:S(2)}, u32[]{:S(2)}) collective-permute-start(f32[384,128]{1,0:T(8,128)} %fusion.89), channel_id=1, source_target_pairs={{0,1},{2,3},{4,5},{6,7},{8,9},{10,11},{12,13},{14,15},{16,17},{18,... | collective-permute-start | bytes 589832 | tf_op jit(solution)/shard_map/ppermute | solution.py:137
  145.7 74.2 %collective-permute-start.39 = (f32[384,128]{1,0:T(8,128)}, f32[384,128]{1,0:T(8,128)}, u32[]{:S(2)}, u32[]{:S(2)}) collective-permute-start(f32[384,128]{1,0:T(8,128)} %fusion.90), channel_id=1, source_target_pairs={{2,1},{4,3},{6,5},{8,7},{10,9},{12,11},{14,13},{16,15},{18,17},{20... | collective-permute-start | bytes 589832 | tf_op jit(solution)/shard_map/ppermute | solution.py:137
  175.1 42.4 %collective-permute-start.5 = (f32[384,384]{1,0:T(8,128)}, f32[384,384]{1,0:T(8,128)S(1)}, u32[]{:S(2)}, u32[]{:S(2)}) collective-permute-start(f32[384,384]{1,0:T(8,128)} %fusion.50), channel_id=1, source_target_pairs={{2,1},{4,3},{6,5},{8,7},{10,9},{12,11},{14,13},{16,15},{18,17},{20... | collective-permute-start | bytes 1769480 | tf_op jit(solution)/shard_map/ppermute | solution.py:137
  182.1 36.5 %collective-permute-start.4 = (f32[384,384]{1,0:T(8,128)}, f32[384,384]{1,0:T(8,128)}, u32[]{:S(2)}, u32[]{:S(2)}) collective-permute-start(f32[384,384]{1,0:T(8,128)} %fusion.49), channel_id=1, source_target_pairs={{0,1},{2,3},{4,5},{6,7},{8,9},{10,11},{12,13},{14,15},{16,17},{18,... | collective-permute-start | bytes 1769480 | tf_op jit(solution)/shard_map/ppermute | solution.py:137
  185.5 28.2 %collective-permute-start.9 = (f32[384,384]{1,0:T(8,128)}, f32[384,384]{1,0:T(8,128)S(1)}, u32[]{:S(2)}, u32[]{:S(2)}) collective-permute-start(f32[384,384]{1,0:T(8,128)} %fusion.56), channel_id=1, source_target_pairs={{0,1},{2,3},{4,5},{6,7},{8,9},{10,11},{12,13},{14,15},{16,17},{18,... | collective-permute-start | bytes 1769480 | tf_op jit(solution)/shard_map/ppermute | solution.py:137
  224.7 53.3 %collective-permute-start.42 = (f32[384,128]{1,0:T(8,128)S(1)}, f32[384,128]{1,0:T(8,128)S(1)}, u32[]{:S(2)}, u32[]{:S(2)}) collective-permute-start(f32[384,128]{1,0:T(8,128)S(1)} %fusion.92), channel_id=1, source_target_pairs={{5,3},{9,7},{13,11},{17,15},{21,19},{25,23},{29,27}} | collective-permute-start | bytes 589832 | tf_op jit(solution)/shard_map/ppermute | solution.py:137
  231.3 42.9 %collective-permute-start.8 = (f32[384,384]{1,0:T(8,128)S(1)}, f32[384,384]{1,0:T(8,128)S(1)}, u32[]{:S(2)}, u32[]{:S(2)}) collective-permute-start(f32[384,384]{1,0:T(8,128)S(1)} %convolution_subtract_fusion.3), channel_id=1, source_target_pairs={{1,3},{5,7},{9,11},{13,15},{17,19},{21,23},{25,27},{29,31}} | collective-permute-start | bytes 1769480 | tf_op jit(solution)/shard_map/ppermute | solution.py:137
  233.3 50.0 %collective-permute-start.14 = (f32[384,384]{1,0:T(8,128)S(1)}, f32[384,384]{1,0:T(8,128)S(1)}, u32[]{:S(2)}, u32[]{:S(2)}) collective-permute-start(f32[384,384]{1,0:T(8,128)S(1)} %fusion.62), channel_id=1, source_target_pairs={{5,3},{9,7},{13,11},{17,15},{21,19},{25,23},{29,27}} | collective-permute-start | bytes 1769480 | tf_op jit(solution)/shard_map/ppermute | solution.py:137
  237.5 41.9 %collective-permute-start.41 = (f32[384,128]{1,0:T(8,128)S(1)}, f32[384,128]{1,0:T(8,128)S(1)}, u32[]{:S(2)}, u32[]{:S(2)}) collective-permute-start(f32[384,128]{1,0:T(8,128)S(1)} %fusion.91), channel_id=1, source_target_pairs={{1,3},{5,7},{9,11},{13,15},{17,19},{21,23},{25,27},{29,31}} | collective-permute-start | bytes 589832 | tf_op jit(solution)/shard_map/ppermute | solution.py:137
  277.9 35.2 %collective-permute-start.12 = (f32[384,384]{1,0:T(8,128)}, f32[384,384]{1,0:T(8,128)}, u32[]{:S(2)}, u32[]{:S(2)}) collective-permute-start(f32[384,384]{1,0:T(8,128)} %fusion.58), channel_id=1, source_target_pairs={{5,3},{9,7},{13,11},{17,15},{21,19},{25,23},{29,27}} | collective-permute-start | bytes 1769480 | tf_op jit(solution)/shard_map/ppermute | solution.py:137
  279.4 33.7 %collective-permute-start.11 = (f32[384,384]{1,0:T(8,128)}, f32[384,384]{1,0:T(8,128)}, u32[]{:S(2)}, u32[]{:S(2)}) collective-permute-start(f32[384,384]{1,0:T(8,128)} %fusion.57), channel_id=1, source_target_pairs={{1,3},{5,7},{9,11},{13,15},{17,19},{21,23},{25,27},{29,31}} | collective-permute-start | bytes 1769480 | tf_op jit(solution)/shard_map/ppermute | solution.py:137
  282.1 44.2 %collective-permute-start.17 = (f32[384,384]{1,0:T(8,128)S(1)}, f32[384,384]{1,0:T(8,128)S(1)}, u32[]{:S(2)}, u32[]{:S(2)}) collective-permute-start(f32[384,384]{1,0:T(8,128)S(1)} %negate_select_fusion.2), channel_id=1, source_target_pairs={{7,3},{15,11},{23,19},{31,27}} | collective-permute-start | bytes 1769480 | tf_op jit(solution)/shard_map/ppermute | solution.py:137
  317.8 48.4 %collective-permute-start.45 = (f32[384,128]{1,0:T(8,128)}, f32[384,128]{1,0:T(8,128)}, u32[]{:S(2)}, u32[]{:S(2)}) collective-permute-start(f32[384,128]{1,0:T(8,128)} %fusion.95), channel_id=1, source_target_pairs={{11,7},{19,15},{27,23}} | collective-permute-start | bytes 589832 | tf_op jit(solution)/shard_map/ppermute | solution.py:137
  332.8 37.8 %collective-permute-start.19 = (f32[384,384]{1,0:T(8,128)}, f32[384,384]{1,0:T(8,128)}, u32[]{:S(2)}, u32[]{:S(2)}) collective-permute-start(f32[384,384]{1,0:T(8,128)} %fusion.66), channel_id=1, source_target_pairs={{11,7},{19,15},{27,23}} | collective-permute-start | bytes 1769480 | tf_op jit(solution)/shard_map/ppermute | solution.py:137
  337.3 28.9 %collective-permute-start.44 = (f32[384,128]{1,0:T(8,128)}, f32[384,128]{1,0:T(8,128)}, u32[]{:S(2)}, u32[]{:S(2)}) collective-permute-start(f32[384,128]{1,0:T(8,128)} %fusion.94), channel_id=1, source_target_pairs={{3,7},{11,15},{19,23},{27,31}} | collective-permute-start | bytes 589832 | tf_op jit(solution)/shard_map/ppermute | solution.py:137
  338.9 31.8 %collective-permute-start.18 = (f32[384,384]{1,0:T(8,128)}, f32[384,384]{1,0:T(8,128)}, u32[]{:S(2)}, u32[]{:S(2)}) collective-permute-start(f32[384,384]{1,0:T(8,128)} %fusion.65), channel_id=1, source_target_pairs={{3,7},{11,15},{19,23},{27,31}} | collective-permute-start | bytes 1769480 | tf_op jit(solution)/shard_map/ppermute | solution.py:137
  340.4 43.0 %collective-permute-start.24 = (f32[384,384]{1,0:T(8,128)S(1)}, f32[384,384]{1,0:T(8,128)S(1)}, u32[]{:S(2)}, u32[]{:S(2)}) collective-permute-start(f32[384,384]{1,0:T(8,128)S(1)} %negate_select_fusion.1), channel_id=1, source_target_pairs={{15,7},{31,23}} | collective-permute-start | bytes 1769480 | tf_op jit(solution)/shard_map/ppermute | solution.py:137
  393.8 36.5 %collective-permute-start.26 = (f32[384,384]{1,0:T(8,128)}, f32[384,384]{1,0:T(8,128)}, u32[]{:S(2)}, u32[]{:S(2)}) collective-permute-start(f32[384,384]{1,0:T(8,128)} %fusion.74), channel_id=1, source_target_pairs={{23,15}} | collective-permute-start | bytes 1769480 | tf_op jit(solution)/shard_map/ppermute | solution.py:137
  395.3 35.0 %collective-permute-start.25 = (f32[384,384]{1,0:T(8,128)}, f32[384,384]{1,0:T(8,128)}, u32[]{:S(2)}, u32[]{:S(2)}) collective-permute-start(f32[384,384]{1,0:T(8,128)} %fusion.73), channel_id=1, source_target_pairs={{7,15},{23,31}} | collective-permute-start | bytes 1769480 | tf_op jit(solution)/shard_map/ppermute | solution.py:137
  398.6 43.5 %collective-permute-start.31 = (f32[384,384]{1,0:T(8,128)S(1)}, f32[384,384]{1,0:T(8,128)}, u32[]{:S(2)}, u32[]{:S(2)}) collective-permute-start(f32[384,384]{1,0:T(8,128)S(1)} %negate_select_fusion), channel_id=1, source_target_pairs={{31,15}} | collective-permute-start | bytes 1769480 | tf_op jit(solution)/shard_map/ppermute | solution.py:137
  433.7 86.9 %collective-permute-start.49 = (f32[384,128]{1,0:T(8,128)}, f32[384,128]{1,0:T(8,128)}, u32[]{:S(2)}, u32[]{:S(2)}) collective-permute-start(f32[384,128]{1,0:T(8,128)} %convolution_subtract_fusion.18), channel_id=1, source_target_pairs={{15,31}} | collective-permute-start | bytes 589832 | tf_op jit(solution)/shard_map/ppermute | solution.py:137
  435.1 82.4 %collective-permute-start.51 = (f32[384,128]{1,0:T(8,128)}, f32[384,128]{1,0:T(8,128)}, u32[]{:S(2)}, u32[]{:S(2)}) collective-permute-start(f32[384,128]{1,0:T(8,128)} %fusion.100), channel_id=1, source_target_pairs={} | collective-permute-start | bytes 589832 | tf_op jit(solution)/shard_map/ppermute | solution.py:137
  450.5 39.7 %collective-permute-start.29 = (f32[384,384]{1,0:T(8,128)}, f32[384,384]{1,0:T(8,128)}, u32[]{:S(2)}, u32[]{:S(2)}) collective-permute-start(f32[384,384]{1,0:T(8,128)} %convolution_subtract_fusion), channel_id=1, source_target_pairs={{15,31}} | collective-permute-start | bytes 1769480 | tf_op jit(solution)/shard_map/ppermute | solution.py:137
  459.2 28.4 %collective-permute-start.32 = (f32[384,384]{1,0:T(8,128)}, f32[384,384]{1,0:T(8,128)}, u32[]{:S(2)}, u32[]{:S(2)}) collective-permute-start(f32[384,384]{1,0:T(8,128)} %fusion.81), channel_id=1, source_target_pairs={{15,31}} | collective-permute-start | bytes 1769480 | tf_op jit(solution)/shard_map/ppermute | solution.py:137
  485.6 31.8 %collective-permute-start.50 = (f32[384,128]{1,0:T(8,128)}, f32[384,128]{1,0:T(8,128)}, u32[]{:S(2)}, u32[]{:S(2)}) collective-permute-start(f32[384,128]{1,0:T(8,128)} %fusion.99), channel_id=1, source_target_pairs={{15,31}} | collective-permute-start | bytes 589832 | tf_op jit(solution)/shard_map/ppermute | solution.py:137
  549.9 63.9 %collective-permute-start.55 = (f32[384,128]{1,0:T(8,128)S(1)}, f32[384,128]{1,0:T(8,128)S(1)}, u32[]{:S(2)}, u32[]{:S(2)}) collective-permute-start(f32[384,128]{1,0:T(8,128)S(1)} %add.163), channel_id=1, source_target_pairs={{3,1},{7,5},{11,9},{15,13},{19,17},{23,21},{27,25},{31,29}} | collective-permute-start | bytes 589832 | tf_op jit(solution)/shard_map/ppermute | solution.py:137
  553.5 61.7 %collective-permute-start.64 = (f32[384,128]{1,0:T(8,128)S(1)}, f32[384,128]{1,0:T(8,128)S(1)}, u32[]{:S(2)}, u32[]{:S(2)}) collective-permute-start(f32[384,128]{1,0:T(8,128)S(1)} %fusion.20), channel_id=1, source_target_pairs={{3,1},{7,5},{11,9},{15,13},{19,17},{23,21},{27,25},{31,29}} | collective-permute-start | bytes 589832 | tf_op jit(solution)/shard_map/ppermute | solution.py:137
  (122 other events, 1386.7 us)
